TPU v7x, 512 devices: a whole 4x8x8 slice. The times are simulated.
512 devices in a mesh: blk: 16 (over z, x_lo), member: 32 (over y, x_hi, core).
Axes of the slice: x: 4 (x_hi: 2, x_lo: 2; x = x_hi * 2 + x_lo), y: 8, z: 8, core: 2. Of those that a mesh axis runs over, the one named last changes fastest.
Arguments:
- tokens: bfloat16 [32, 32, 4096], P('member', 'blk'), may hold values from -6 to 6
- cotangent: bfloat16 [32, 32, 4096], P('member', 'blk'), may hold values from -6 to 6
- routes: int32 [32, 32, 8], P('member'), may hold values from 0 to 63, all different within a row; in each aligned block of 32 rows (0 to 31, 32 to 63, ..., all dimensions but the last counted through in order) at most 6 rows name the same one
- gate_wts: float32 [32, 32, 8], P('member'), may hold values from 0.2 to 1
- w_gate: bfloat16 [16, 4096, 4096], P('blk', 'member'), may hold values from -0.09375 to 0.09375
- w_up: bfloat16 [16, 4096, 4096], P('blk', 'member'), may hold values from -0.09375 to 0.09375
- w_down: bfloat16 [16, 4096, 4096], P('blk', 'member'), may hold values from -0.1875 to 0.1875
Outputs:
- layer_out: bfloat16 [32, 32, 4096], P('member', 'blk')
- grad_in: bfloat16 [32, 32, 4096], P('member', 'blk')
Inputs may be any that keep to these rules, and one draw needn't show every extreme that they name: `routes`: each token names 8 different experts. Within one token column (the 32 tokens of one index of the first dimension) no expert is named by more than 6 tokens, and in every draw some expert is named by exactly 6 tokens of some column.
All inputs are finite; a program needn't handle non-finite values.
Results may differ from a plain program's by a relative error of at most 0.0058.
Values may be sent and summed in bfloat16 or wider, within the bound.
A program may use at most 64 MiB of HBM per device.

v0:
```python
import jax
import jax.numpy as jnp
from jax import lax
from jax.sharding import PartitionSpec as P

EXP_GRP = 4
CAP = 6


CONTRACT_LAST = (((1,), (1,)), ((), ()))
CONTRACT_FIRST = (((0,), (0,)), ((), ()))


def slot_layout(route_ids, first_expert, capacity):
    local_ids = route_ids - first_expert
    slot_ids = jnp.arange(EXP_GRP, dtype=jnp.int32)
    matches = (local_ids[None, :, :] == slot_ids[:, None, None]).astype(jnp.int32)
    running = jnp.cumsum(matches.reshape(EXP_GRP, -1), axis=1).reshape(matches.shape) - 1
    places = jnp.arange(capacity, dtype=jnp.int32)
    chosen = (matches[:, None, :, :] == 1) & (running[:, None, :, :] == places[None, :, None, None])
    return chosen.astype(jnp.float32)


def expert_forward(row_block, gate_local, up_local, down_local):
    pre_gate = lax.dot_general(
        row_block, gate_local, CONTRACT_LAST, preferred_element_type=jnp.float32
    )
    pre_up = lax.dot_general(row_block, up_local, CONTRACT_LAST, preferred_element_type=jnp.float32)
    hidden = (pre_gate * jax.nn.sigmoid(pre_gate) * pre_up).astype(jnp.bfloat16)
    partial_value = jnp.dot(hidden, down_local, preferred_element_type=jnp.float32).astype(
        jnp.bfloat16
    )
    return (partial_value, pre_gate, pre_up)


def expert_backward(cot_rows, pre_gate, pre_up, gate_local, up_local, down_local):
    d_hidden = lax.dot_general(
        cot_rows, down_local, CONTRACT_LAST, preferred_element_type=jnp.float32
    )
    logistic = jax.nn.sigmoid(pre_gate)
    activated = pre_gate * logistic
    grad_gate = (d_hidden * pre_up * logistic * (1.0 + pre_gate * (1.0 - logistic))).astype(
        jnp.bfloat16
    )
    grad_up = (d_hidden * activated).astype(jnp.bfloat16)
    partial_value = jnp.dot(grad_gate, gate_local, preferred_element_type=jnp.float32)
    partial_value = partial_value + jnp.dot(grad_up, up_local, preferred_element_type=jnp.float32)
    return partial_value.astype(jnp.bfloat16)


def combine_rows(occupied, slot_weight, returned, shards):
    model_width = returned.shape[2]
    per_slot = jnp.sum(
        returned.astype(jnp.float32).reshape(EXP_GRP, shards, -1, model_width), axis=1
    )
    scaled = per_slot.reshape(-1, model_width) * slot_weight
    return lax.dot_general(
        occupied,
        scaled,
        CONTRACT_FIRST,
        precision=lax.Precision.HIGHEST,
        preferred_element_type=jnp.float32,
    )


def body(tokens, cotangent, routes, gate_wts, w_gate, w_up, w_down):
    col_x, col_g = (
        lax.all_gather(tokens[0], "blk", axis=0, tiled=True),
        lax.all_gather(cotangent[0], "blk", axis=0, tiled=True),
    )
    model_width = col_x.shape[1]
    members = lax.axis_size("member")
    shards = members // EXP_GRP
    layout = slot_layout(routes[0], lax.axis_index("blk") * EXP_GRP, CAP)
    occupied = jnp.sum(layout, axis=3).reshape(EXP_GRP * CAP, -1)
    picker = occupied.astype(jnp.bfloat16)
    slot_weight = jnp.sum(layout * gate_wts[0][None, None, :, :], axis=(2, 3)).reshape(
        EXP_GRP * CAP, 1
    )
    send_x = jnp.dot(picker, col_x, preferred_element_type=jnp.float32).astype(jnp.bfloat16)
    send_g = jnp.dot(picker, col_g, preferred_element_type=jnp.float32).astype(jnp.bfloat16)
    send_x = jnp.repeat(send_x.reshape(EXP_GRP, CAP, model_width), shards, axis=0)
    send_g = jnp.repeat(send_g.reshape(EXP_GRP, CAP, model_width), shards, axis=0)
    gate_local = w_gate[0]
    up_local = w_up[0]
    down_local = w_down[0]
    arrived_x = lax.all_to_all(send_x, "member", split_axis=0, concat_axis=0, tiled=True)
    out_part, pre_gate, pre_up = expert_forward(
        arrived_x.reshape(-1, model_width), gate_local, up_local, down_local
    )
    back_out = lax.all_to_all(
        out_part.reshape(members, CAP, model_width),
        "member",
        split_axis=0,
        concat_axis=0,
        tiled=True,
    )
    arrived_g = lax.all_to_all(send_g, "member", split_axis=0, concat_axis=0, tiled=True)
    grad_part = expert_backward(
        arrived_g.reshape(-1, model_width), pre_gate, pre_up, gate_local, up_local, down_local
    )
    back_grad = lax.all_to_all(
        grad_part.reshape(members, CAP, model_width),
        "member",
        split_axis=0,
        concat_axis=0,
        tiled=True,
    )
    summed_out = combine_rows(occupied, slot_weight, back_out, shards)
    summed_grad = combine_rows(occupied, slot_weight, back_grad, shards)
    out_rows, grad_rows = (
        lax.psum_scatter(summed_out, "blk", scatter_dimension=0, tiled=True),
        lax.psum_scatter(summed_grad, "blk", scatter_dimension=0, tiled=True),
    )
    return (out_rows.astype(jnp.bfloat16)[None], grad_rows.astype(jnp.bfloat16)[None])


def solution(mesh):
    placed = (
        P("member", "blk", None),
        P("member", "blk", None),
        P("member", None, None),
        P("member", None, None),
        P("blk", "member", None),
        P("blk", "member", None),
        P("blk", "member", None),
    )
    return jax.shard_map(
        body,
        mesh=mesh,
        in_specs=placed,
        out_specs=(P("member", "blk", None), P("member", "blk", None)),
        check_vma=False,
    )
```

profile of v0, /device:TPU:12, one launch (start us, length us, event | category | flops | bytes accessed | tf_op | source)
XLA Modules:
  0.0 370.1 jit_solution(18091575036808248603)
XLA Ops:
  0.6 0.0 copy-start
  0.6 0.8 broadcast_subtract_fusion
  1.4 0.1 copy.32
  1.5 0.1 eq.58
  1.6 1.2 reduce-window.6
  2.8 0.1 reshape.89
  2.9 0.1 slice.8
  3.0 0.7 fusion.36
  3.7 0.1 copy.33
  3.8 0.1 copy.34
  3.9 0.1 broadcast.43
  4.0 0.1 reshape.91
  4.1 0.1 add_add_fusion
  4.2 0.1 copy.35
  4.3 0.9 select_reduce_fusion
  5.2 0.7 copy.36
  5.9 42.3 %all-gather = bf16[1,32,4096]{2,0,1:T(2,128)(2,1)S(1)} all-gather(bf16[1,2,4096]{2,0,1:T(2,128)(2,1)S(1)} %copy.36), channel_id=2, replica_groups=mesh['blk'=16,'member'=32] {'blk'}, dimensions={1}, use_global_device_ids=true | all-gather | bytes 278528 | tf_op jit(solution)/shard_map/all_gather | solution.py:68
  48.2 0.4 convolution_convert_fusion.2
  48.6 0.1 reshape.92
  48.7 1.6 broadcast_in_dim.8
  50.3 0.0 copy-start.4
  50.3 10.2 %all-to-all-start = ((bf16[32,6,4096]{2,1,0:T(8,128)(2,1)}), bf16[32,6,4096]{2,1,0:T(8,128)(2,1)S(1)}, u32[]{:S(2)}, u32[]{:S(2)}) async-start(bf16[32,6,4096]{2,1,0:T(8,128)(2,1)} %bitcast.49), calls=%async_computation | async-start | bytes 4194304 | tf_op jit(solution)/shard_map/all_to_all | solution.py:87
  60.5 0.0 copy-done.4
  60.6 36.6 %all-gather.1 = bf16[1,32,4096]{2,0,1:T(2,128)(2,1)S(1)} all-gather(bf16[1,2,4096]{2,0,1:T(2,128)(2,1)S(1)} %copy.37), channel_id=3, replica_groups=mesh['blk'=16,'member'=32] {'blk'}, dimensions={1}, use_global_device_ids=true | all-gather | bytes 278528 | tf_op jit(solution)/shard_map/all_gather | solution.py:69
  97.2 1.1 convolution_convert_fusion.1
  98.2 1.0 reshape.98
  99.2 11.8 %all-to-all-done = bf16[32,6,4096]{2,1,0:T(8,128)(2,1)S(1)} async-done(((bf16[32,6,4096]{2,1,0:T(8,128)(2,1)}), bf16[32,6,4096]{2,1,0:T(8,128)(2,1)S(1)}, u32[]{:S(2)}, u32[]{:S(2)}) %all-to-all-start) | async-done | bytes 1572896 | tf_op jit(solution)/shard_map/all_to_all | solution.py:87
  111.0 0.0 copy-start.1
  111.0 1.8 broadcast_in_dim.19
  112.8 0.2 copy-done.1
  113.1 6.0 %all-to-all-start.2 = ((bf16[32,6,4096]{2,1,0:T(8,128)(2,1)}), bf16[32,6,4096]{2,1,0:T(8,128)(2,1)}, u32[]{:S(2)}, u32[]{:S(2)}) async-start(bf16[32,6,4096]{2,1,0:T(8,128)(2,1)} %bitcast.50), calls=%async_computation.2 | async-start | bytes 4194304 | tf_op jit(solution)/shard_map/all_to_all | solution.py:98
  119.0 2.6 reshape.94
  121.6 0.0 copy-done
  121.6 0.0 copy-start.2
  121.6 0.6 fusion.9
  122.2 0.6 copy-done.2
  122.8 0.6 fusion.5
  123.4 46.2 %all-to-all-done.2 = bf16[32,6,4096]{2,1,0:T(8,128)(2,1)} async-done(((bf16[32,6,4096]{2,1,0:T(8,128)(2,1)}), bf16[32,6,4096]{2,1,0:T(8,128)(2,1)}, u32[]{:S(2)}, u32[]{:S(2)}) %all-to-all-start.2) | async-done | bytes 1572896 | tf_op jit(solution)/shard_map/all_to_all | solution.py:98
  169.6 2.5 reshape.100
  172.2 1.8 fusion.1
  174.0 0.0 copy-start.3
  174.0 0.6 fusion.7
  174.6 0.6 copy-done.3
  175.2 0.6 fusion
  175.8 1.6 reshape.101
  177.3 5.9 %all-to-all-start.3 = ((bf16[32,6,4096]{2,1,0:T(8,128)(2,1)}), bf16[32,6,4096]{2,1,0:T(8,128)(2,1)S(1)}, u32[]{:S(2)}, u32[]{:S(2)}) async-start(bf16[32,6,4096]{2,1,0:T(8,128)(2,1)} %reshape.101), calls=%async_computation.3 | async-start | bytes 4194304 | tf_op jit(solution)/shard_map/all_to_all | solution.py:102
  183.2 3.0 convolution_convert_fusion
  186.2 3.5 reshape.95
  189.7 44.1 %all-to-all-done.3 = bf16[32,6,4096]{2,1,0:T(8,128)(2,1)S(1)} async-done(((bf16[32,6,4096]{2,1,0:T(8,128)(2,1)}), bf16[32,6,4096]{2,1,0:T(8,128)(2,1)S(1)}, u32[]{:S(2)}, u32[]{:S(2)}) %all-to-all-start.3) | async-done | bytes 1572896 | tf_op jit(solution)/shard_map/all_to_all | solution.py:102
  233.8 5.9 %all-to-all-start.1 = ((bf16[32,6,4096]{2,1,0:T(8,128)(2,1)}), bf16[32,6,4096]{2,1,0:T(8,128)(2,1)}, u32[]{:S(2)}, u32[]{:S(2)}) async-start(bf16[32,6,4096]{2,1,0:T(8,128)(2,1)} %reshape.95), calls=%async_computation.1 | async-start | bytes 4194304 | tf_op jit(solution)/shard_map/all_to_all | solution.py:91
  239.7 1.3 dynamic-slice
  241.7 0.5 convert_reduce_fusion
  242.1 0.8 convolution_bitcast_fusion
  242.9 47.4 %all-to-all-done.1 = bf16[32,6,4096]{2,1,0:T(8,128)(2,1)} async-done(((bf16[32,6,4096]{2,1,0:T(8,128)(2,1)}), bf16[32,6,4096]{2,1,0:T(8,128)(2,1)}, u32[]{:S(2)}, u32[]{:S(2)}) %all-to-all-start.1) | async-done | bytes 1572896 | tf_op jit(solution)/shard_map/all_to_all | solution.py:91
  290.3 2.1 convert_reduce_fusion.1
  292.4 0.8 convolution_bitcast_fusion.1
  293.2 76.2 %all-reduce.4 = (bf16[32,4096]{1,0:T(8,128)(2,1)S(1)}, bf16[32,4096]{1,0:T(8,128)(2,1)S(1)}) all-reduce(f32[32,4096]{1,0:T(8,128)S(1)} %convolution_bitcast_fusion.1, f32[32,4096]{1,0:T(8,128)S(1)} %convolution_bitcast_fusion), channel_id=4, replica_groups=mesh['blk'=16,'member'=32] {'blk'}, use_global_device_ids=true, to_apply=%region_5.6.clone | all-reduce | flops 262144 | bytes 1572864
  369.4 0.7 fusion.24
  (7 shorter events, 0.1 us)
Async XLA Ops:
  0.6 121.0 %copy-start = (bf16[1,128,4096]{2,1,0:T(8,128)(2,1)S(1)}, bf16[1,128,4096]{2,1,0:T(8,128)(2,1)}, u32[]{:S(2)}) copy-start(bf16[1,128,4096]{2,1,0:T(8,128)(2,1)} %param.11) | copy-start | bytes 3145732
  50.3 10.3 %copy-start.4 = (bf16[1,2,4096]{2,1,0:T(2,128)(2,1)S(1)}, bf16[1,2,4096]{2,1,0:T(2,128)(2,1)}, u32[]{:S(2)}) copy-start(bf16[1,2,4096]{2,1,0:T(2,128)(2,1)} %param.8) | copy-start | bytes 49156
  50.3 60.8 %all-to-all-start = ((bf16[32,6,4096]{2,1,0:T(8,128)(2,1)}), bf16[32,6,4096]{2,1,0:T(8,128)(2,1)S(1)}, u32[]{:S(2)}, u32[]{:S(2)}) async-start(bf16[32,6,4096]{2,1,0:T(8,128)(2,1)} %bitcast.49), calls=%async_computation | async-start | bytes 4194304 | tf_op jit(solution)/shard_map/all_to_all | solution.py:87
  111.0 2.0 copy-start.1
  113.1 56.5 %all-to-all-start.2 = ((bf16[32,6,4096]{2,1,0:T(8,128)(2,1)}), bf16[32,6,4096]{2,1,0:T(8,128)(2,1)}, u32[]{:S(2)}, u32[]{:S(2)}) async-start(bf16[32,6,4096]{2,1,0:T(8,128)(2,1)} %bitcast.50), calls=%async_computation.2 | async-start | bytes 4194304 | tf_op jit(solution)/shard_map/all_to_all | solution.py:98
  121.6 1.2 copy-start.2
  174.0 1.2 copy-start.3
  177.3 56.4 %all-to-all-start.3 = ((bf16[32,6,4096]{2,1,0:T(8,128)(2,1)}), bf16[32,6,4096]{2,1,0:T(8,128)(2,1)S(1)}, u32[]{:S(2)}, u32[]{:S(2)}) async-start(bf16[32,6,4096]{2,1,0:T(8,128)(2,1)} %reshape.101), calls=%async_computation.3 | async-start | bytes 4194304 | tf_op jit(solution)/shard_map/all_to_all | solution.py:102
  233.8 56.5 %all-to-all-start.1 = ((bf16[32,6,4096]{2,1,0:T(8,128)(2,1)}), bf16[32,6,4096]{2,1,0:T(8,128)(2,1)}, u32[]{:S(2)}, u32[]{:S(2)}) async-start(bf16[32,6,4096]{2,1,0:T(8,128)(2,1)} %reshape.95), calls=%async_computation.1 | async-start | bytes 4194304 | tf_op jit(solution)/shard_map/all_to_all | solution.py:91
where the time goes:
time: 371 us; the launch traced here: 370 us
  blocking collectives  155 us (42%)
  waiting for transfers between devices  149 us (40%)
  starting transfers between devices  28 us (8%)
  local copies, waits for them, and re-layouts  19.7 us (5%)
  matrix products  10.1 us (3%)
  other arithmetic  6.26 us (2%)
    unnamed x1, blocking collectives  76.2 us
    all_to_all x1, waiting for transfers between devices, body(): lax.all_to_all(out_part.reshape(members, CAP, model_width), 'member', spl...  47.4 us
    all_to_all x1, waiting for transfers between devices, body(): lax.all_to_all(send_g, 'member', split_axis=0, concat_axis=0, tiled=True)  46.2 us
    all_to_all x1, waiting for transfers between devices, body(): lax.all_to_all(grad_part.reshape(members, CAP, model_width), 'member', sp...  44.1 us
    all_gather x1, blocking collectives, body(): lax.all_gather(tokens[0], 'blk', axis=0, tiled=True)  42.3 us
    all_gather x1, blocking collectives, body(): lax.all_gather(cotangent[0], 'blk', axis=0, tiled=True)  36.6 us
    all_to_all x1, waiting for transfers between devices, body(): lax.all_to_all(send_x, 'member', split_axis=0, concat_axis=0, tiled=True)  11.8 us
    all_to_all x1, starting transfers between devices, body(): lax.all_to_all(send_x, 'member', split_axis=0, concat_axis=0, tiled=True)  10.2 us
  transfers between devices with their start and end apart: 4, of which 4 were waited for; matrix products, arithmetic and copies ran while one was open for 4% of the time, Pallas kernels for 0%

commit v1 on v0

v1 whole, which is shorter than its diff:
```python
import functools

import jax
import jax.numpy as jnp
import numpy as np
from jax import lax
from jax.experimental import pallas as pl
from jax.experimental.pallas import tpu as pltpu
from jax.sharding import PartitionSpec as P

MESH = pl.DeviceIdType.MESH
EXP_GRP = 4
CAP = 6
PAD = 8
SHARDS = 8
COLS = 32
BLKS = 16
BF = jnp.bfloat16
F32 = jnp.float32
NT = (((1,), (1,)), ((), ()))
VMEM_SPEC = pl.BlockSpec(memory_space=pltpu.VMEM)
CHUNKS = 4


def loop(start, stop, step):
    def run(k, carry):
        step(k)
        return carry

    lax.fori_loop(start, stop, run, 0)


def greet(axis, me, n):
    barrier = pltpu.get_barrier_semaphore()
    loop(
        1,
        n,
        lambda k: pl.semaphore_signal(
            barrier, inc=1, device_id={axis: lax.rem(me + k, n)}, device_id_type=MESH
        ),
    )
    pl.semaphore_wait(barrier, n - 1)


def send(src, dst, send_sem, recv_sem, axis, peer):
    return pltpu.make_async_remote_copy(
        src_ref=src,
        dst_ref=dst,
        send_sem=send_sem,
        recv_sem=recv_sem,
        device_id={axis: peer},
        device_id_type=MESH,
    )


def flip(m, w):
    return m + w - 2 * w * lax.rem(m // w, 2)


def gather_kernel(x, g, out, send_sem, recv_sem):
    me = lax.axis_index("blk")
    greet("blk", me, BLKS)

    def copies(k):
        peer = lax.rem(me + k, BLKS)
        return [
            send(src.at[0], out.at[me, h], send_sem.at[h, k], recv_sem.at[h, k], "blk", peer)
            for h, src in enumerate((x, g))
        ]

    loop(1, BLKS, lambda k: [c.start() for c in copies(k)])
    out[me, 0] = x[0]
    out[me, 1] = g[0]
    loop(1, BLKS, lambda k: [c.wait() for c in copies(k)])


def swap_kernel(src, out, send_sem, recv_sem):
    me = lax.axis_index("blk")
    greet("blk", me, BLKS)

    def copy(k):
        peer = lax.rem(me + k, BLKS)
        return send(src.at[peer], out.at[me], send_sem.at[k], recv_sem.at[k], "blk", peer)

    loop(1, BLKS, lambda k: copy(k).start())
    out[me] = src[me]
    loop(1, BLKS, lambda k: copy(k).wait())


def dispatch_kernel(src, out, send_sem, recv_sem, own_sem, hop_send, hop_recv):
    me = lax.axis_index("member")
    width = src.shape[1] // SHARDS
    rows = 2 * PAD
    mine = lax.rem(me, SHARDS)
    greet("member", me, COLS)

    def piece(peer):
        return src.at[
            pl.ds(pl.multiple_of(rows * (peer // SHARDS), rows), rows),
            pl.ds(pl.multiple_of(width * lax.rem(peer, SHARDS), width), width),
        ]

    def place(col, part):
        return out.at[
            pl.ds(pl.multiple_of(rows * col, rows), rows),
            pl.ds(pl.multiple_of(width * part, width), width),
        ]

    def put(k):
        peer = lax.rem(me + k, COLS)
        return send(
            piece(peer),
            place(me, lax.rem(peer, SHARDS)),
            send_sem.at[k],
            recv_sem.at[me],
            "member",
            peer,
        )

    own = pltpu.make_async_copy(piece(me), place(me, mine), own_sem)
    loop(1, COLS, lambda k: put(k).start())
    own.start()

    per = COLS // CHUNKS
    tall = rows * per

    def hop(kind, q, origin, peer):
        part = out.at[
            pl.ds(tall * q, tall), pl.ds(pl.multiple_of(width * origin, width), width)
        ]
        return send(part, part, hop_send.at[kind, q], hop_recv.at[kind, q], "member", peer)

    across, along, other = flip(me, 2), flip(me, 4), flip(me, 1)
    part_x, part_y = flip(mine, 2), flip(mine, 4)
    part_xy = flip(part_x, 4)

    def arrived(c):
        @pl.when(c != me)
        def _():
            send(
                place(c, mine), place(c, mine), send_sem.at[0], recv_sem.at[c], "member", other
            ).wait_recv()

    own.wait()
    to_x = [hop(0, q, mine, across) for q in range(CHUNKS)]
    to_y = [hop(1, q, mine, along) for q in range(CHUNKS)]
    pass_y = [hop(2, q, part_x, along) for q in range(CHUNKS)]
    core = [
        [hop(3 + i, q, origin, other) for q in range(CHUNKS)]
        for i, origin in enumerate((mine, part_x, part_y, part_xy))
    ]
    for q in range(CHUNKS):
        loop(per * q, per * (q + 1), arrived)
        to_x[q].start()
        to_y[q].start()
        core[0][q].start()
    for q in range(CHUNKS):
        to_x[q].wait_recv()
        pass_y[q].start()
        core[1][q].start()
    for q in range(CHUNKS):
        to_y[q].wait_recv()
        core[2][q].start()
    for q in range(CHUNKS):
        pass_y[q].wait_recv()
        core[3][q].start()
    loop(1, COLS, lambda k: put(k).wait_send())
    for q in range(CHUNKS):
        for c in (to_x[q], to_y[q], pass_y[q]):
            c.wait_send()
        for i in range(4):
            core[i][q].wait()


def expert_kernel(rows_ref, gate, up, down, pack_o, pack_g, out, acc):
    depth = 512

    acc[...] = jnp.zeros_like(acc)

    def first(k, carry):
        cols = pl.ds(pl.multiple_of(depth * k, depth), depth)
        left = rows_ref[:, cols]
        for i, w in enumerate((gate, up, down)):
            acc[i] += lax.dot_general(left, w[:, cols], NT, preferred_element_type=F32)
        return carry

    lax.fori_loop(0, rows_ref.shape[1] // depth, first, 0)
    n = gate.shape[0]
    split = [acc[i].reshape(COLS, 2, PAD, n) for i in range(3)]
    pre_gate = split[0][:, 0].reshape(COLS * PAD, n)
    pre_up = split[1][:, 0].reshape(COLS * PAD, n)
    d_hidden = split[2][:, 1].reshape(COLS * PAD, n)
    logistic = jax.nn.sigmoid(pre_gate)
    activated = pre_gate * logistic
    hidden = (activated * pre_up).astype(BF)
    grad_gate = (d_hidden * pre_up * logistic * (1.0 + pre_gate * (1.0 - logistic))).astype(BF)
    grad_up = (d_hidden * activated).astype(BF)
    lhs_d = jnp.dot(pack_o[...], hidden, preferred_element_type=F32).astype(BF)
    lhs_g = jnp.dot(pack_g[...], grad_gate, preferred_element_type=F32).astype(BF)
    lhs_u = jnp.dot(pack_g[...], grad_up, preferred_element_type=F32).astype(BF)

    def second(k, carry):
        cols = pl.ds(pl.multiple_of(depth * k, depth), depth)
        total = jnp.dot(lhs_d, down[:, cols], preferred_element_type=F32)
        total += jnp.dot(lhs_g, gate[:, cols], preferred_element_type=F32)
        total += jnp.dot(lhs_u, up[:, cols], preferred_element_type=F32)
        out[:, cols] = total.astype(BF)
        return carry

    lax.fori_loop(0, rows_ref.shape[1] // depth, second, 0)


def collect_kernel(
    og, unpack, out, t1, s1, t2, s2, t3, home, c_send, c_recv, y_send, y_recv, x_send, x_recv,
    h_send, h_recv, own_sem,
):
    me = lax.axis_index("member")
    width = og.shape[1] // SHARDS
    mine = lax.rem(me, SHARDS)
    bit_c, bit_x, bit_y = lax.rem(me, 2), lax.rem(me // 2, 2), lax.rem(me // 4, 2)
    across, along, other = flip(me, 2), flip(me, 4), flip(me, 1)
    tall = og.shape[0] // CHUNKS
    per = COLS // CHUNKS
    rows = 2 * PAD
    greet("member", me, COLS)

    def span(q):
        return pl.ds(tall * q, tall)

    def lanes(part):
        return pl.ds(pl.multiple_of(width * part, width), width)

    def swap_core(q, h):
        return send(
            og.at[span(q), lanes(2 * h + 1 - bit_c)],
            t1.at[h, span(q)],
            c_send.at[q, h],
            c_recv.at[q, h],
            "member",
            other,
        )

    def swap_y(q, i):
        return send(
            s1.at[2 * (1 - bit_y) + i, span(q)],
            t2.at[i, span(q)],
            y_send.at[q, i],
            y_recv.at[q, i],
            "member",
            along,
        )

    def swap_x(q):
        return send(
            s2.at[1 - bit_x, span(q)], t3.at[span(q)], x_send.at[q], x_recv.at[q], "member", across
        )

    def spot(source):
        return out.at[
            pl.ds(pl.multiple_of(rows * (source // SHARDS), rows), rows),
            lanes(lax.rem(source, SHARDS)),
        ]

    def deliver(c):
        return send(
            home.at[pl.ds(pl.multiple_of(rows * c, rows), rows)],
            spot(me),
            h_send.at[c],
            h_recv.at[me],
            "member",
            c,
        )

    def others(step):
        def run(c):
            @pl.when(c != me)
            def _():
                step(c)

        return run

    for q in range(CHUNKS):
        for h in range(4):
            swap_core(q, h).start()
    for q in range(CHUNKS):
        for h in range(4):
            swap_core(q, h).wait_recv()
            total = og[span(q), lanes(2 * h + bit_c)].astype(F32) + t1[h, span(q)].astype(F32)
            s1[h, span(q)] = total.astype(BF)
        for i in range(2):
            swap_y(q, i).start()
    for q in range(CHUNKS):
        for i in range(2):
            swap_y(q, i).wait_recv()
            total = s1[2 * bit_y + i, span(q)].astype(F32) + t2[i, span(q)].astype(F32)
            s2[i, span(q)] = total.astype(BF)
        swap_x(q).start()
    for q in range(CHUNKS):
        swap_x(q).wait_recv()
        total = s2[bit_x, span(q)].astype(F32) + t3[span(q)].astype(F32)
        wide = jnp.dot(unpack[...], total.astype(BF), preferred_element_type=F32)
        home[pl.ds(rows * per * q, rows * per)] = wide.astype(BF)
        loop(per * q, per * (q + 1), others(lambda c: deliver(c).start()))
    own = pltpu.make_async_copy(
        home.at[pl.ds(pl.multiple_of(rows * me, rows), rows)], spot(me), own_sem
    )
    own.start()
    for q in range(CHUNKS):
        for h in range(4):
            swap_core(q, h).wait_send()
        for i in range(2):
            swap_y(q, i).wait_send()
        swap_x(q).wait_send()
    loop(0, COLS, others(lambda c: deliver(c).wait_send()))

    def landed(c):
        send(
            home.at[pl.ds(0, rows)], spot(c), h_send.at[0], h_recv.at[c], "member", other
        ).wait_recv()

    loop(0, COLS, others(landed))
    own.wait()


def remote_call(kernel, n_in, shape, scratch, ident):
    return pl.pallas_call(
        kernel,
        out_shape=jax.ShapeDtypeStruct(shape, BF),
        in_specs=[VMEM_SPEC] * n_in,
        out_specs=VMEM_SPEC,
        scratch_shapes=scratch,
        compiler_params=pltpu.CompilerParams(collective_id=ident, has_side_effects=True),
    )


def packing():
    pack = np.zeros((2, COLS * 2 * CAP, COLS * PAD), np.float32)
    unpack = np.zeros((COLS // CHUNKS * 2 * PAD, COLS // CHUNKS * 2 * CAP), np.float32)
    for c in range(COLS):
        for h in range(2):
            for r in range(CAP):
                pack[h, (c * 2 + h) * CAP + r, c * PAD + r] = 1
                if c < COLS // CHUNKS:
                    unpack[(c * 2 + h) * PAD + r, (c * 2 + h) * CAP + r] = 1
    return jnp.asarray(pack[0], BF), jnp.asarray(pack[1], BF), jnp.asarray(unpack, BF)


def body(tokens, cotangent, routes, gate_wts, w_gate, w_up, w_down):
    width = tokens.shape[2]
    dma = pltpu.SemaphoreType.DMA
    pack_o, pack_g, unpack = packing()

    experts = lax.axis_index("blk") * EXP_GRP + jnp.arange(EXP_GRP, dtype=jnp.int32)
    match = routes[0][None] == experts[:, None, None]
    named = jnp.sum(match.astype(F32), axis=2)
    weight = jnp.sum(jnp.where(match, gate_wts[0][None], 0.0), axis=2)
    earlier = np.tril(np.ones((COLS, COLS), np.float32), -1)
    rank = jnp.sum(named[:, None, :] * earlier[None], axis=2)
    places = jnp.arange(PAD, dtype=jnp.int32).astype(F32)
    taken = jnp.where(
        (rank[:, None, :] == places[None, :, None]) & (named[:, None, :] > 0), 1.0, 0.0
    )
    both = np.eye(2, dtype=np.float32)[None, :, None, None, :, None]

    def table(values):
        grid = values.reshape(EXP_GRP, 1, PAD, BLKS, 1, COLS // BLKS) * both
        return grid.reshape(EXP_GRP * 2 * PAD, 2 * COLS)

    picker = table(taken).astype(BF)
    combine = table(taken * weight[:, None, :]).T

    column = remote_call(
        gather_kernel,
        2,
        (BLKS, 2, COLS // BLKS, width),
        [dma((2, BLKS)), dma((2, BLKS))],
        0,
    )(tokens, cotangent)
    picked = jnp.dot(
        picker, column.reshape(2 * COLS, width), preferred_element_type=F32
    ).astype(BF)
    arrived = remote_call(
        dispatch_kernel,
        1,
        (COLS * 2 * PAD, width),
        [dma((COLS,)), dma((COLS,)), dma(()), dma((7, CHUNKS)), dma((7, CHUNKS))],
        1,
    )(picked)
    part = pl.pallas_call(
        expert_kernel,
        out_shape=jax.ShapeDtypeStruct((COLS * 2 * CAP, width), BF),
        in_specs=[VMEM_SPEC] * 6,
        out_specs=VMEM_SPEC,
        scratch_shapes=[pltpu.VMEM((3, COLS * 2 * PAD, w_gate.shape[1]), F32)],
    )(arrived, w_gate[0], w_up[0], w_down[0], pack_o, pack_g)
    dense, piece = COLS * 2 * CAP, width // SHARDS
    sums = remote_call(
        collect_kernel,
        2,
        (EXP_GRP * 2 * PAD, width),
        [
            pltpu.VMEM((4, dense, piece), BF),
            pltpu.VMEM((4, dense, piece), BF),
            pltpu.VMEM((2, dense, piece), BF),
            pltpu.VMEM((2, dense, piece), BF),
            pltpu.VMEM((dense, piece), BF),
            pltpu.VMEM((COLS * 2 * PAD, piece), BF),
            dma((CHUNKS, 4)),
            dma((CHUNKS, 4)),
            dma((CHUNKS, 2)),
            dma((CHUNKS, 2)),
            dma((CHUNKS,)),
            dma((CHUNKS,)),
            dma((COLS,)),
            dma((COLS,)),
            dma(()),
        ],
        2,
    )(part, unpack)
    mixed = jnp.dot(
        combine, sums.astype(F32), precision=lax.Precision.HIGHEST, preferred_element_type=F32
    ).astype(BF)
    shares = remote_call(
        swap_kernel,
        1,
        (BLKS, 2, COLS // BLKS, width),
        [dma((BLKS,)), dma((BLKS,))],
        3,
    )(mixed.reshape(BLKS, 2, COLS // BLKS, width))
    final = jnp.sum(shares.astype(F32), axis=0).astype(BF)
    return final[0][None], final[1][None]


def solution(mesh):
    placed = (
        P("member", "blk", None),
        P("member", "blk", None),
        P("member", None, None),
        P("member", None, None),
        P("blk", "member", None),
        P("blk", "member", None),
        P("blk", "member", None),
    )
    return jax.shard_map(
        body,
        mesh=mesh,
        in_specs=placed,
        out_specs=(P("member", "blk", None), P("member", "blk", None)),
        check_vma=False,
    )
```

time: 371 us -> 170 us (0.46)
  the two profiles are of different devices: /device:TPU:12 before, /device:TPU:62 now
where the time goes in v1:
time: 170 us; the launch traced here: 169 us
  Pallas kernels  157 us (92%)
  other arithmetic  4.21 us (2%)
  local copies, waits for them, and re-layouts  3.94 us (2%)
  matrix products  2.72 us (2%)
    pallas_call x1, Pallas kernels, body(): remote_call(dispatch_kernel, 1, (COLS * 2 * PAD, width), [dma((COLS,)), d...  49.3 us
    pallas_call x1, Pallas kernels, body(): remote_call(collect_kernel, 2, (EXP_GRP * 2 * PAD, width), [pltpu.VMEM((4...  47.3 us
    pallas_call x1, Pallas kernels, body(): remote_call(gather_kernel, 2, (BLKS, 2, COLS // BLKS, width), [dma((2, BL...  25.9 us
    pallas_call x1, Pallas kernels, body(): remote_call(swap_kernel, 1, (BLKS, 2, COLS // BLKS, width), [dma((BLKS,))...  21.5 us
    pallas_call x1, Pallas kernels, body(): pl.pallas_call(expert_kernel, out_shape=jax.ShapeDtypeStruct((COLS * 2 *...  13.4 us

profile of v1, /device:TPU:62, one launch (start us, length us, event | category | flops | bytes accessed | tf_op | source)
XLA Modules:
  0.0 169.1 jit_solution(3119230304869892237)
XLA Ops:
  0.7 0.8 fusion
  1.5 0.8 multiply_reduce_fusion
  2.3 0.1 gt.16
  2.4 0.2 copy.22
  2.6 0.1 copy.21
  2.7 0.1 copy.23
  2.8 0.2 and_select_fusion
  3.0 0.9 multiply_convert_fusion
  3.9 0.1 convert_element_type.34
  4.0 0.3 mul.82
  4.3 25.9 %shard_map.131 = bf16[16,2,2,4096]{3,2,1,0:T(2,128)(2,1)} custom-call(bf16[1,2,4096]{2,1,0:T(2,128)(2,1)} %x.1, bf16[1,2,4096]{2,1,0:T(2,128)(2,1)} %g.1), custom_call_target="tpu_custom_call" | custom-call | tf_op jit(solution)/shard_map/pallas_call | solution.py:372
  30.2 1.2 reshape.70
  31.4 1.1 convolution_convert_fusion.1.src
  32.5 49.3 %shard_map.132.rows_ref = bf16[512,4096]{1,0:T(8,128)(2,1)} custom-call(bf16[64,4096]{1,0:T(8,128)(2,1)} %convolution_convert_fusion.1.src), custom_call_target="tpu_custom_call" | custom-call | tf_op jit(solution)/shard_map/pallas_call | solution.py:382
  81.9 13.4 %shard_map.133.og = bf16[384,4096]{1,0:T(8,128)(2,1)} custom-call(bf16[512,4096]{1,0:T(8,128)(2,1)} %shard_map.132.rows_ref, bf16[128,4096]{1,0:T(8,128)(2,1)} %bitcast.15, bf16[128,4096]{1,0:T(8,128)(2,1)} %bitcast.16, bf16[128,4096]{1,0:T(8,128)(2,1)} %bitcast.17, bf16[384,256]{1,0:T(8,128)(2,1)} %constant.25.clone.pack_o, ...), custom_call_target="tpu_custom_call" | custom-call | tf_op jit(solution)/shard_map/pallas_call | solution.py:389
  95.3 47.3 %shard_map.134 = bf16[64,4096]{1,0:T(8,128)(2,1)} custom-call(bf16[384,4096]{1,0:T(8,128)(2,1)} %shard_map.133.og, bf16[128,96]{1,0:T(8,128)(2,1)} %constant.27.clone.unpack), custom_call_target="tpu_custom_call" | custom-call | tf_op jit(solution)/shard_map/pallas_call | solution.py:397
  142.6 1.6 convolution_convert_fusion
  144.2 1.1 reshape.71.src
  145.4 21.5 %shard_map.135 = bf16[16,2,2,4096]{3,2,1,0:T(2,128)(2,1)} custom-call(bf16[16,2,2,4096]{3,2,1,0:T(2,128)(2,1)} %reshape.71.src), custom_call_target="tpu_custom_call" | custom-call | tf_op jit(solution)/shard_map/pallas_call | solution.py:423
  166.9 1.5 reduce_sum.42
  168.4 0.6 fusion.2
  (3 shorter events, 0.0 us)

commit v2 on v1

v2 whole, which is shorter than its diff:
```python
import jax
import jax.numpy as jnp
import numpy as np
from jax import lax
from jax.experimental import pallas as pl
from jax.experimental.pallas import tpu as pltpu
from jax.sharding import PartitionSpec as P

MESH = pl.DeviceIdType.MESH
EXP_GRP = 4
CAP = 6
PAD = 8
SHARDS = 8
COLS = 32
BLKS = 16
BF = jnp.bfloat16
F32 = jnp.float32
NT = (((1,), (1,)), ((), ()))
VMEM_SPEC = pl.BlockSpec(memory_space=pltpu.VMEM)
CHUNKS = 4


def loop(start, stop, step):
    def run(k, carry):
        step(k)
        return carry

    lax.fori_loop(start, stop, run, 0)


def greet(axis, me, n):
    barrier = pltpu.get_barrier_semaphore()
    loop(
        1,
        n,
        lambda k: pl.semaphore_signal(
            barrier, inc=1, device_id={axis: lax.rem(me + k, n)}, device_id_type=MESH
        ),
    )
    pl.semaphore_wait(barrier, n - 1)


def send(src, dst, send_sem, recv_sem, axis, peer):
    return pltpu.make_async_remote_copy(
        src_ref=src,
        dst_ref=dst,
        send_sem=send_sem,
        recv_sem=recv_sem,
        device_id={axis: peer},
        device_id_type=MESH,
    )


def flip(m, w):
    return m + w - 2 * w * lax.rem(m // w, 2)


def greet_few(axis, peers):
    barrier = pltpu.get_barrier_semaphore()
    for peer in peers:
        pl.semaphore_signal(barrier, inc=1, device_id={axis: peer}, device_id_type=MESH)
    pl.semaphore_wait(barrier, len(peers))


FAR_FIRST = (4, 3, 5, 2, 6, 1, 7)
NEAR_FIRST = (1, 7, 2, 6, 3, 5, 4)


def gather_kernel(x, g, out, send_sem, recv_sem, pass_send, pass_recv):
    me = lax.axis_index("blk")
    partner = flip(me, 1)
    ahead = {k: lax.rem(me + 2 * k, BLKS) for k in range(1, 8)}
    greet_few("blk", [ahead[k] for k in FAR_FIRST] + [partner])

    def first(k, peer):
        return [
            send(src.at[0], out.at[me, h], send_sem.at[h, k], recv_sem.at[h, k], "blk", peer)
            for h, src in enumerate((x, g))
        ]

    def passed(k, source):
        return send(
            out.at[source], out.at[source], pass_send.at[k], pass_recv.at[k], "blk", partner
        )

    direct = {k: first(k, ahead[k]) for k in FAR_FIRST}
    direct[0] = first(0, partner)
    for k in FAR_FIRST + (0,):
        for c in direct[k]:
            c.start()
    out[me, 0] = x[0]
    out[me, 1] = g[0]
    relays = []
    for k in NEAR_FIRST:
        for c in direct[k]:
            c.wait_recv()
        relay = passed(k, lax.rem(me + BLKS - 2 * k, BLKS))
        relay.start()
        relays.append(relay)
    for c in direct[0]:
        c.wait_recv()
    for k in FAR_FIRST + (0,):
        for c in direct[k]:
            c.wait_send()
    for relay in relays:
        relay.wait()


def swap_kernel(src, out_a, out_b, near, mid, far, send_sem, recv_sem, far_send, far_recv):
    me = lax.axis_index("blk")
    partner = flip(me, 1)
    ahead = {k: lax.rem(me + 2 * k, BLKS) for k in range(8)}
    greet_few("blk", [ahead[k] for k in FAR_FIRST] + [partner])

    def pair(k):
        return send(
            src.at[flip(ahead[k], 1)],
            near.at[flip(ahead[k], 1) // 2],
            send_sem.at[k],
            recv_sem.at[k],
            "blk",
            partner,
        )

    def along(k):
        return send(mid.at[k], far.at[k], far_send.at[k], far_recv.at[k], "blk", ahead[k])

    order = FAR_FIRST + (0,)
    for k in order:
        pair(k).start()
    for k in order:
        pair(k).wait_recv()
        total = src[ahead[k]].astype(F32) + near[ahead[k] // 2].astype(F32)
        if k:
            mid[k] = total.astype(BF)
            along(k).start()
    for k in NEAR_FIRST:
        along(k).wait_recv()
        total = total + far[k].astype(F32)
    out_a[0] = total[0].astype(BF)
    out_b[0] = total[1].astype(BF)
    for k in order:
        pair(k).wait_send()
        if k:
            along(k).wait_send()


def layer_kernel(
    src, gate, up, down, pack, unpack, out,
    rows_ref, w, acc, og, t1, s1, t2, s2, t3, home,
    send_sem, recv_sem, own_sem, w_sem, hop_send, hop_recv,
    c_send, c_recv, y_send, y_recv, x_send, x_recv, h_send, h_recv,
):
    me = lax.axis_index("member")
    width = src.shape[1] // SHARDS
    rows = 2 * PAD
    dense = 2 * CAP
    per = COLS // CHUNKS
    mine = lax.rem(me, SHARDS)
    bit_c, bit_x, bit_y = lax.rem(me, 2), lax.rem(me // 2, 2), lax.rem(me // 4, 2)
    across, along, other = flip(me, 2), flip(me, 4), flip(me, 1)
    part_x, part_y = flip(mine, 2), flip(mine, 4)
    part_xy = flip(part_x, 4)

    loads = [
        pltpu.make_async_copy(ref.at[0], w.at[i], w_sem.at[i])
        for i, ref in enumerate((gate, up, down))
    ]
    for load in loads:
        load.start()
    greet("member", me, COLS)

    def some(size, at):
        return pl.ds(pl.multiple_of(size * at, size), size)

    def lanes(part):
        return some(width, part)

    def piece(peer):
        return src.at[some(rows, peer // SHARDS), lanes(lax.rem(peer, SHARDS))]

    def place(col, part):
        return rows_ref.at[some(rows, col), lanes(part)]

    def put(k):
        peer = lax.rem(me + k, COLS)
        return send(
            piece(peer),
            place(me, lax.rem(peer, SHARDS)),
            send_sem.at[k],
            recv_sem.at[me],
            "member",
            peer,
        )

    def others(step):
        def run(c):
            @pl.when(c != me)
            def _():
                step(c)

        return run

    def arrived(c):
        send(
            place(c, mine), place(c, mine), send_sem.at[0], recv_sem.at[c], "member", other
        ).wait_recv()

    def hop(kind, q, origin, peer):
        part = rows_ref.at[some(rows * per, q), lanes(origin)]
        return send(part, part, hop_send.at[kind, q], hop_recv.at[kind, q], "member", peer)

    to_x = lambda q: hop(0, q, mine, across)
    to_y = lambda q: hop(1, q, mine, along)
    pass_y = lambda q: hop(2, q, part_x, along)
    origins = (mine, part_x, part_y, part_xy)
    core = lambda i, q: hop(3 + i, q, origins[i], other)

    def multiply(q, origin, fresh=False):
        span, cols = some(rows * per, q), lanes(origin)
        left = rows_ref[span, cols]
        for i in range(3):
            term = lax.dot_general(left, w[i, :, cols], NT, preferred_element_type=F32)
            acc[i, span] = term if fresh else acc[i, span] + term

    own = pltpu.make_async_copy(piece(me), place(me, mine), own_sem.at[0])
    loop(1, COLS, lambda k: put(k).start())
    own.start()
    own.wait()

    def phase_own(q):
        loop(per * q, per * (q + 1), others(arrived))
        to_x(q).start()
        to_y(q).start()
        core(0, q).start()

    def phase_x(q):
        to_x(q).wait_recv()
        pass_y(q).start()
        core(1, q).start()
        multiply(q, part_x)

    def phase_y(q):
        to_y(q).wait_recv()
        core(2, q).start()
        multiply(q, part_y)

    def phase_core(q):
        for i in range(3):
            core(i, q).wait_recv()
            multiply(q, flip(origins[i], 1))

    def swap_core(q, h):
        return send(
            og.at[some(dense * per, q), lanes(2 * h + 1 - bit_c)],
            t1.at[h, some(dense * per, q)],
            c_send.at[q, h],
            c_recv.at[q, h],
            "member",
            other,
        )

    def finish(q):
        pass_y(q).wait_recv()
        core(3, q).start()
        multiply(q, part_xy)
        core(3, q).wait_recv()
        multiply(q, flip(part_xy, 1))
        n = w.shape[1]
        split = [acc[i, some(rows * per, q)].reshape(per, 2, PAD, n) for i in range(3)]
        pre_gate = split[0][:, 0].reshape(per * PAD, n)
        pre_up = split[1][:, 0].reshape(per * PAD, n)
        d_hidden = split[2][:, 1].reshape(per * PAD, n)
        logistic = jax.nn.sigmoid(pre_gate)
        activated = pre_gate * logistic
        hidden = (activated * pre_up).astype(BF)
        grad_gate = (
            d_hidden * pre_up * logistic * (1.0 + pre_gate * (1.0 - logistic))
        ).astype(BF)
        grad_up = (d_hidden * activated).astype(BF)
        left = [
            jnp.dot(pack[h], v, preferred_element_type=F32).astype(BF)
            for h, v in ((1, grad_gate), (1, grad_up), (0, hidden))
        ]

        def second(k):
            cols = lanes(k)
            total = jnp.dot(left[0], w[0, :, cols], preferred_element_type=F32)
            total += jnp.dot(left[1], w[1, :, cols], preferred_element_type=F32)
            total += jnp.dot(left[2], w[2, :, cols], preferred_element_type=F32)
            og[some(dense * per, q), cols] = total.astype(BF)

        loop(0, SHARDS, second)
        for h in range(4):
            swap_core(q, h).start()

    loop(0, CHUNKS, phase_own)
    for load in loads:
        load.wait()
    loop(0, CHUNKS, lambda q: multiply(q, mine, True))
    loop(0, CHUNKS, phase_x)
    loop(0, CHUNKS, phase_y)
    loop(0, CHUNKS, phase_core)
    loop(0, CHUNKS, finish)

    def span(q):
        return some(dense * per, q)

    def swap_y(q, i):
        return send(
            s1.at[2 * (1 - bit_y) + i, span(q)],
            t2.at[i, span(q)],
            y_send.at[q, i],
            y_recv.at[q, i],
            "member",
            along,
        )

    def swap_x(q):
        return send(
            s2.at[1 - bit_x, span(q)], t3.at[span(q)], x_send.at[q], x_recv.at[q], "member", across
        )

    def spot(source):
        return out.at[some(rows, source // SHARDS), lanes(lax.rem(source, SHARDS))]

    def deliver(c):
        return send(
            home.at[some(rows, c)], spot(me), h_send.at[c], h_recv.at[me], "member", c
        )

    def add_core(q):
        for h in range(4):
            swap_core(q, h).wait_recv()
            total = og[span(q), lanes(2 * h + bit_c)].astype(F32) + t1[h, span(q)].astype(F32)
            s1[h, span(q)] = total.astype(BF)
        for i in range(2):
            swap_y(q, i).start()

    def add_y(q):
        for i in range(2):
            swap_y(q, i).wait_recv()
            total = s1[2 * bit_y + i, span(q)].astype(F32) + t2[i, span(q)].astype(F32)
            s2[i, span(q)] = total.astype(BF)
        swap_x(q).start()

    def add_x(q):
        swap_x(q).wait_recv()
        total = s2[bit_x, span(q)].astype(F32) + t3[span(q)].astype(F32)
        wide = jnp.dot(unpack[...], total.astype(BF), preferred_element_type=F32)
        home[some(rows * per, q)] = wide.astype(BF)
        loop(per * q, per * (q + 1), others(lambda c: deliver(c).start()))

    loop(0, CHUNKS, add_core)
    loop(0, CHUNKS, add_y)
    loop(0, CHUNKS, add_x)
    last = pltpu.make_async_copy(home.at[some(rows, me)], spot(me), own_sem.at[1])
    last.start()

    def drain(q):
        to_x(q).wait_send()
        to_y(q).wait_send()
        pass_y(q).wait_send()
        for i in range(4):
            core(i, q).wait_send()
            swap_core(q, i).wait_send()
        for i in range(2):
            swap_y(q, i).wait_send()
        swap_x(q).wait_send()

    def landed(c):
        send(
            home.at[some(rows, 0)], spot(c), h_send.at[0], h_recv.at[c], "member", other
        ).wait_recv()

    loop(1, COLS, lambda k: put(k).wait_send())
    loop(0, CHUNKS, drain)
    loop(0, COLS, others(lambda c: deliver(c).wait_send()))
    loop(0, COLS, others(landed))
    last.wait()


def remote_call(kernel, specs, shape, scratch, ident):
    return pl.pallas_call(
        kernel,
        out_shape=jax.tree.map(lambda dims: jax.ShapeDtypeStruct(dims, BF), shape,
                               is_leaf=lambda v: isinstance(v[0], int)),
        in_specs=specs,
        out_specs=jax.tree.map(lambda dims: VMEM_SPEC, shape,
                               is_leaf=lambda v: isinstance(v[0], int)),
        scratch_shapes=scratch,
        compiler_params=pltpu.CompilerParams(collective_id=ident, has_side_effects=True),
    )


def packing():
    per = COLS // CHUNKS
    pack = np.zeros((2, per * 2 * CAP, per * PAD), np.float32)
    unpack = np.zeros((per * 2 * PAD, per * 2 * CAP), np.float32)
    for c in range(per):
        for h in range(2):
            for r in range(CAP):
                pack[h, (c * 2 + h) * CAP + r, c * PAD + r] = 1
                unpack[(c * 2 + h) * PAD + r, (c * 2 + h) * CAP + r] = 1
    return jnp.asarray(pack, BF), jnp.asarray(unpack, BF)


def body(tokens, cotangent, routes, gate_wts, w_gate, w_up, w_down):
    width = tokens.shape[2]
    dma = pltpu.SemaphoreType.DMA
    pack, unpack = packing()

    experts = lax.axis_index("blk") * EXP_GRP + jnp.arange(EXP_GRP, dtype=jnp.int32)
    match = routes[0][None] == experts[:, None, None]
    named = jnp.sum(match.astype(F32), axis=2)
    weight = jnp.sum(jnp.where(match, gate_wts[0][None], 0.0), axis=2)
    earlier = np.tril(np.ones((COLS, COLS), np.float32), -1)
    rank = jnp.sum(named[:, None, :] * earlier[None], axis=2)
    places = jnp.arange(PAD, dtype=jnp.int32).astype(F32)
    taken = jnp.where(
        (rank[:, None, :] == places[None, :, None]) & (named[:, None, :] > 0), 1.0, 0.0
    )
    both = np.eye(2, dtype=np.float32)[None, :, None, None, :, None]

    def table(values):
        grid = values.reshape(EXP_GRP, 1, PAD, BLKS, 1, COLS // BLKS) * both
        return grid.reshape(EXP_GRP * 2 * PAD, 2 * COLS)

    picker = table(taken).astype(BF)
    combine = table(taken * weight[:, None, :]).T

    pairs = COLS // BLKS
    column = remote_call(
        gather_kernel,
        [VMEM_SPEC] * 2,
        (BLKS, 2, pairs, width),
        [dma((2, 8)), dma((2, 8)), dma((8,)), dma((8,))],
        0,
    )(tokens, cotangent)
    picked = jnp.dot(
        picker, column.reshape(2 * COLS, width), preferred_element_type=F32
    ).astype(BF)
    dense, padded, piece = COLS * 2 * CAP, COLS * 2 * PAD, width // SHARDS
    hidden = w_gate.shape[1]
    sums = remote_call(
        layer_kernel,
        [VMEM_SPEC] + [pl.BlockSpec(memory_space=pl.ANY)] * 3 + [VMEM_SPEC] * 2,
        (EXP_GRP * 2 * PAD, width),
        [
            pltpu.VMEM((padded, width), BF),
            pltpu.VMEM((3, hidden, width), BF),
            pltpu.VMEM((3, padded, hidden), F32),
            pltpu.VMEM((dense, width), BF),
            pltpu.VMEM((4, dense, piece), BF),
            pltpu.VMEM((4, dense, piece), BF),
            pltpu.VMEM((2, dense, piece), BF),
            pltpu.VMEM((2, dense, piece), BF),
            pltpu.VMEM((dense, piece), BF),
            pltpu.VMEM((padded, piece), BF),
            dma((COLS,)),
            dma((COLS,)),
            dma((2,)),
            dma((3,)),
            dma((7, CHUNKS)),
            dma((7, CHUNKS)),
            dma((CHUNKS, 4)),
            dma((CHUNKS, 4)),
            dma((CHUNKS, 2)),
            dma((CHUNKS, 2)),
            dma((CHUNKS,)),
            dma((CHUNKS,)),
            dma((COLS,)),
            dma((COLS,)),
        ],
        1,
    )(picked, w_gate, w_up, w_down, pack, unpack)
    mixed = jnp.dot(
        combine, sums.astype(F32), precision=lax.Precision.HIGHEST, preferred_element_type=F32
    ).astype(BF)
    half = (BLKS // 2, 2, pairs, width)
    return remote_call(
        swap_kernel,
        [VMEM_SPEC],
        ((1, pairs, width), (1, pairs, width)),
        [pltpu.VMEM(half, BF)] * 3 + [dma((8,))] * 4,
        2,
    )(mixed.reshape(BLKS, 2, pairs, width))


def solution(mesh):
    placed = (
        P("member", "blk", None),
        P("member", "blk", None),
        P("member", None, None),
        P("member", None, None),
        P("blk", "member", None),
        P("blk", "member", None),
        P("blk", "member", None),
    )
    return jax.shard_map(
        body,
        mesh=mesh,
        in_specs=placed,
        out_specs=(P("member", "blk", None), P("member", "blk", None)),
        check_vma=False,
    )
```

time: 170 us -> 148 us (0.87)
  the two profiles are of different devices: /device:TPU:62 before, /device:TPU:58 now
where the time goes in v2:
time: 148 us; the launch traced here: 147 us
  Pallas kernels  136 us (92%)
  local copies, waits for them, and re-layouts  6.58 us (4%)
  matrix products  2.71 us (2%)
    pallas_call x1, Pallas kernels, body(): remote_call(layer_kernel, [VMEM_SPEC] + [pl.BlockSpec(memory_space=pl.ANY...  93 us
    pallas_call x1, Pallas kernels, body(): remote_call(gather_kernel, [VMEM_SPEC] * 2, (BLKS, 2, pairs, width), [dma...  25.5 us
    pallas_call x1, Pallas kernels, body(): remote_call(swap_kernel, [VMEM_SPEC], ((1, pairs, width), (1, pairs, widt...  18 us
    unnamed x12, local copies, waits for them, and re-layouts  3.28 us

profile of v2, /device:TPU:58, one launch (start us, length us, event | category | flops | bytes accessed | tf_op | source)
XLA Modules:
  0.0 147.1 jit_solution(14910495173816085033)
XLA Ops:
  0.6 0.0 copy-start.2
  0.6 0.0 copy-start.3
  0.7 0.0 copy-start
  0.7 0.6 copy-done.2
  1.3 0.0 copy-done.3
  1.3 0.1 fusion
  1.4 0.0 copy-done
  1.4 0.1 multiply_reduce_fusion
  1.5 0.1 gt.16
  1.6 0.2 copy.21
  1.9 0.1 copy.20
  1.9 0.1 copy.22
  2.0 0.2 and_select_fusion
  2.2 0.0 copy-start.4
  2.2 0.7 copy-done.4
  2.9 0.2 multiply_convert_fusion
  3.1 0.1 convert_element_type.32
  3.3 0.3 mul.82
  3.6 25.5 %shard_map.122 = bf16[16,2,2,4096]{3,2,1,0:T(2,128)(2,1)} custom-call(bf16[1,2,4096]{2,1,0:T(2,128)(2,1)} %x.1, bf16[1,2,4096]{2,1,0:T(2,128)(2,1)} %g.1), custom_call_target="tpu_custom_call" | custom-call | tf_op jit(solution)/shard_map/pallas_call | solution.py:433
  29.1 1.2 reshape.70
  30.3 1.1 convolution_convert_fusion.1.src
  31.4 93.0 %shard_map.123 = bf16[64,4096]{1,0:T(8,128)(2,1)} custom-call(bf16[64,4096]{1,0:T(8,128)(2,1)} %convolution_convert_fusion.1.src, bf16[1,128,4096]{2,1,0:T(8,128)(2,1)} %gate.1, bf16[1,128,4096]{2,1,0:T(8,128)(2,1)} %up.1, bf16[1,128,4096]{2,1,0:T(8,128)(2,1)} %down.1, bf16[2,96,64]{2,1,0:T(8,128)(2,1)} %constant.21.clone.pack, ...), custom_call_target="tpu_custom_call" | custom-call | tf_op jit(solution)/shard_map/pallas_call | solution.py:445
  124.4 1.6 %convolution_convert_fusion = bf16[64,4096]{1,0:T(8,128)(2,1)S(1)} fusion(f32[64,64]{0,1:T(8,128)S(1)} %mul.82, bf16[64,4096]{1,0:T(8,128)(2,1)} %shard_map.123), kind=kOutput, calls=%fused_computation | convolution fusion | flops 201588736 | bytes 1064960 | tf_op jit(solution)/shard_map/dot_general | solution.py:477
  126.0 1.1 reshape.71.src
  127.1 18.0 %shard_map.124 = (bf16[1,2,4096]{2,1,0:T(2,128)(2,1)}, bf16[1,2,4096]{2,1,0:T(2,128)(2,1)}) custom-call(bf16[16,2,2,4096]{3,2,1,0:T(2,128)(2,1)} %reshape.71.src), custom_call_target="tpu_custom_call" | custom-call | tf_op jit(solution)/shard_map/pallas_call | solution.py:481
  145.1 0.0 copy-start.1
  145.1 1.3 copy.25
  146.5 0.0 copy-done.1
  146.5 0.6 copy.26
  (3 shorter events, 0.0 us)
Async XLA Ops:
  0.6 0.7 copy-start.2
  0.6 0.7 copy-start.3
  0.7 0.8 copy-start
  2.2 0.7 copy-start.4
  145.1 1.4 copy-start.1

commit v3 on v2

--- a/solution.py
+++ b/solution.py
@@ -212,7 +212,12 @@
 
     to_x = lambda q: hop(0, q, mine, across)
     to_y = lambda q: hop(1, q, mine, along)
-    pass_y = lambda q: hop(2, q, part_x, along)
+
+    def route(q, relay_y, relay_x):
+        late = (q + CHUNKS - 1) // CHUNKS
+        return (1 - late) * relay_y + late * relay_x
+
+    relay = lambda q: hop(2, q, route(q, part_x, part_y), route(q, along, across))
     origins = (mine, part_x, part_y, part_xy)
     core = lambda i, q: hop(3 + i, q, origins[i], other)
 
@@ -234,15 +239,13 @@
         to_y(q).start()
         core(0, q).start()
 
-    def phase_x(q):
+    def phase_near(q):
         to_x(q).wait_recv()
-        pass_y(q).start()
         core(1, q).start()
+        to_y(q).wait_recv()
+        relay(q).start()
+        core(2, q).start()
         multiply(q, part_x)
-
-    def phase_y(q):
-        to_y(q).wait_recv()
-        core(2, q).start()
         multiply(q, part_y)
 
     def phase_core(q):
@@ -261,7 +264,7 @@
         )
 
     def finish(q):
-        pass_y(q).wait_recv()
+        relay(q).wait_recv()
         core(3, q).start()
         multiply(q, part_xy)
         core(3, q).wait_recv()
@@ -298,27 +301,31 @@
     for load in loads:
         load.wait()
     loop(0, CHUNKS, lambda q: multiply(q, mine, True))
-    loop(0, CHUNKS, phase_x)
-    loop(0, CHUNKS, phase_y)
+    loop(0, CHUNKS, phase_near)
     loop(0, CHUNKS, phase_core)
-    loop(0, CHUNKS, finish)
+    finish(0)
 
     def span(q):
         return some(dense * per, q)
 
-    def swap_y(q, i):
-        return send(
-            s1.at[2 * (1 - bit_y) + i, span(q)],
+    def swap_pair(q, i):
+        return send(
+            s1.at[route(q, 2 * (1 - bit_y) + i, 2 * i + 1 - bit_x), span(q)],
             t2.at[i, span(q)],
             y_send.at[q, i],
             y_recv.at[q, i],
             "member",
-            along,
-        )
-
-    def swap_x(q):
-        return send(
-            s2.at[1 - bit_x, span(q)], t3.at[span(q)], x_send.at[q], x_recv.at[q], "member", across
+            route(q, along, across),
+        )
+
+    def swap_last(q):
+        return send(
+            s2.at[1 - route(q, bit_x, bit_y), span(q)],
+            t3.at[span(q)],
+            x_send.at[q],
+            x_recv.at[q],
+            "member",
+            route(q, across, along),
         )
 
     def spot(source):
@@ -335,38 +342,43 @@
             total = og[span(q), lanes(2 * h + bit_c)].astype(F32) + t1[h, span(q)].astype(F32)
             s1[h, span(q)] = total.astype(BF)
         for i in range(2):
-            swap_y(q, i).start()
-
-    def add_y(q):
+            swap_pair(q, i).start()
+
+    def add_pair(q):
         for i in range(2):
-            swap_y(q, i).wait_recv()
-            total = s1[2 * bit_y + i, span(q)].astype(F32) + t2[i, span(q)].astype(F32)
-            s2[i, span(q)] = total.astype(BF)
-        swap_x(q).start()
-
-    def add_x(q):
-        swap_x(q).wait_recv()
-        total = s2[bit_x, span(q)].astype(F32) + t3[span(q)].astype(F32)
+            swap_pair(q, i).wait_recv()
+            kept = s1[route(q, 2 * bit_y + i, 2 * i + bit_x), span(q)]
+            s2[i, span(q)] = (kept.astype(F32) + t2[i, span(q)].astype(F32)).astype(BF)
+        swap_last(q).start()
+
+    def add_last(q):
+        swap_last(q).wait_recv()
+        total = s2[route(q, bit_x, bit_y), span(q)].astype(F32) + t3[span(q)].astype(F32)
         wide = jnp.dot(unpack[...], total.astype(BF), preferred_element_type=F32)
         home[some(rows * per, q)] = wide.astype(BF)
         loop(per * q, per * (q + 1), others(lambda c: deliver(c).start()))
 
-    loop(0, CHUNKS, add_core)
-    loop(0, CHUNKS, add_y)
-    loop(0, CHUNKS, add_x)
+    def step(q):
+        finish(q)
+        add_core(q - 1)
+
+    loop(1, CHUNKS, step)
+    add_core(CHUNKS - 1)
+    loop(0, CHUNKS, add_pair)
+    loop(0, CHUNKS, add_last)
     last = pltpu.make_async_copy(home.at[some(rows, me)], spot(me), own_sem.at[1])
     last.start()
 
     def drain(q):
         to_x(q).wait_send()
         to_y(q).wait_send()
-        pass_y(q).wait_send()
+        relay(q).wait_send()
         for i in range(4):
             core(i, q).wait_send()
             swap_core(q, i).wait_send()
         for i in range(2):
-            swap_y(q, i).wait_send()
-        swap_x(q).wait_send()
+            swap_pair(q, i).wait_send()
+        swap_last(q).wait_send()
 
     def landed(c):
         send(

time: 148 us -> 141 us (0.953)
  Pallas kernels: 136 us -> 130 us
    pallas_call x1, Pallas kernels: 93 us -> 86.7 us  [body(): remote_call(layer_kernel, [VMEM_SPEC] + [pl.BlockSpec(memory_space=pl.ANY...]
where the time goes in v3:
time: 141 us
  Pallas kernels  130 us (92%)
  local copies, waits for them, and re-layouts  6.58 us (5%)
  matrix products  2.69 us (2%)
    pallas_call x1, Pallas kernels, body(): remote_call(layer_kernel, [VMEM_SPEC] + [pl.BlockSpec(memory_space=pl.ANY...  86.7 us
    pallas_call x1, Pallas kernels, body(): remote_call(gather_kernel, [VMEM_SPEC] * 2, (BLKS, 2, pairs, width), [dma...  25.5 us
    pallas_call x1, Pallas kernels, body(): remote_call(swap_kernel, [VMEM_SPEC], ((1, pairs, width), (1, pairs, widt...  18.2 us
    unnamed x12, local copies, waits for them, and re-layouts  3.28 us

profile of v3, /device:TPU:58, one launch (start us, length us, event | category | flops | bytes accessed | tf_op | source)
XLA Modules:
  0.0 141.0 jit_solution(3421292521906204322)
XLA Ops:
  0.6 0.0 copy-start.2
  0.6 0.0 copy-start.3
  0.7 0.0 copy-start
  0.7 0.6 copy-done.2
  1.3 0.0 copy-done.3
  1.3 0.1 fusion
  1.4 0.0 copy-done
  1.4 0.1 multiply_reduce_fusion
  1.5 0.1 gt.16
  1.6 0.2 copy.21
  1.9 0.1 copy.20
  1.9 0.1 copy.22
  2.0 0.2 and_select_fusion
  2.2 0.0 copy-start.4
  2.2 0.7 copy-done.4
  2.9 0.2 multiply_convert_fusion
  3.1 0.1 convert_element_type.32
  3.3 0.3 mul.82
  3.6 25.5 %shard_map.122 = bf16[16,2,2,4096]{3,2,1,0:T(2,128)(2,1)} custom-call(bf16[1,2,4096]{2,1,0:T(2,128)(2,1)} %x.1, bf16[1,2,4096]{2,1,0:T(2,128)(2,1)} %g.1), custom_call_target="tpu_custom_call" | custom-call | tf_op jit(solution)/shard_map/pallas_call | solution.py:445
  29.1 1.2 reshape.70
  30.3 1.1 convolution_convert_fusion.1.src
  31.4 86.7 %shard_map.123 = bf16[64,4096]{1,0:T(8,128)(2,1)} custom-call(bf16[64,4096]{1,0:T(8,128)(2,1)} %convolution_convert_fusion.1.src, bf16[1,128,4096]{2,1,0:T(8,128)(2,1)} %gate.1, bf16[1,128,4096]{2,1,0:T(8,128)(2,1)} %up.1, bf16[1,128,4096]{2,1,0:T(8,128)(2,1)} %down.1, bf16[2,96,64]{2,1,0:T(8,128)(2,1)} %constant.21.clone.pack, ...), custom_call_target="tpu_custom_call" | custom-call | tf_op jit(solution)/shard_map/pallas_call | solution.py:457
  118.1 1.6 %convolution_convert_fusion = bf16[64,4096]{1,0:T(8,128)(2,1)S(1)} fusion(f32[64,64]{0,1:T(8,128)S(1)} %mul.82, bf16[64,4096]{1,0:T(8,128)(2,1)} %shard_map.123), kind=kOutput, calls=%fused_computation | convolution fusion | flops 201588736 | bytes 1064960 | tf_op jit(solution)/shard_map/dot_general | solution.py:489
  119.7 1.1 reshape.71.src
  120.8 18.2 %shard_map.124 = (bf16[1,2,4096]{2,1,0:T(2,128)(2,1)}, bf16[1,2,4096]{2,1,0:T(2,128)(2,1)}) custom-call(bf16[16,2,2,4096]{3,2,1,0:T(2,128)(2,1)} %reshape.71.src), custom_call_target="tpu_custom_call" | custom-call | tf_op jit(solution)/shard_map/pallas_call | solution.py:493
  139.0 0.0 copy-start.1
  139.0 1.3 copy.25
  140.4 0.0 copy-done.1
  140.4 0.6 copy.26
  (3 shorter events, 0.0 us)
Async XLA Ops:
  0.6 0.7 copy-start.2
  0.6 0.7 copy-start.3
  0.7 0.8 copy-start
  2.2 0.7 copy-start.4
  139.0 1.4 copy-start.1

commit v4 on v3

--- a/solution.py
+++ b/solution.py
@@ -182,8 +182,16 @@
     def place(col, part):
         return rows_ref.at[some(rows, col), lanes(part)]
 
+    slot = me // SHARDS
+
+    def chunk(q):
+        return lax.rem(slot + q + (q // 2) * (1 - 2 * (q % 2)), CHUNKS)
+
+    def column(q, j):
+        return per * chunk(q) + j
+
     def put(k):
-        peer = lax.rem(me + k, COLS)
+        peer = column(k // per, lax.rem(mine + k, per))
         return send(
             piece(peer),
             place(me, lax.rem(peer, SHARDS)),
@@ -207,7 +215,7 @@
         ).wait_recv()
 
     def hop(kind, q, origin, peer):
-        part = rows_ref.at[some(rows * per, q), lanes(origin)]
+        part = rows_ref.at[some(rows * per, chunk(q)), lanes(origin)]
         return send(part, part, hop_send.at[kind, q], hop_recv.at[kind, q], "member", peer)
 
     to_x = lambda q: hop(0, q, mine, across)
@@ -223,7 +231,7 @@
 
     def multiply(q, origin, fresh=False):
         span, cols = some(rows * per, q), lanes(origin)
-        left = rows_ref[span, cols]
+        left = rows_ref[some(rows * per, chunk(q)), cols]
         for i in range(3):
             term = lax.dot_general(left, w[i, :, cols], NT, preferred_element_type=F32)
             acc[i, span] = term if fresh else acc[i, span] + term
@@ -234,7 +242,7 @@
     own.wait()
 
     def phase_own(q):
-        loop(per * q, per * (q + 1), others(arrived))
+        loop(0, per, lambda j: others(arrived)(column(q, j)))
         to_x(q).start()
         to_y(q).start()
         core(0, q).start()
@@ -331,10 +339,14 @@
     def spot(source):
         return out.at[some(rows, source // SHARDS), lanes(lax.rem(source, SHARDS))]
 
-    def deliver(c):
-        return send(
-            home.at[some(rows, c)], spot(me), h_send.at[c], h_recv.at[me], "member", c
-        )
+    def deliver(q, j):
+        c = column(q, j)
+        return send(
+            home.at[some(rows, per * q + j)], spot(me), h_send.at[c], h_recv.at[me], "member", c
+        )
+
+    def deliver_all(q, step):
+        loop(0, per, lambda j: others(lambda c: step(deliver(q, j)))(column(q, j)))
 
     def add_core(q):
         for h in range(4):
@@ -356,7 +368,7 @@
         total = s2[route(q, bit_x, bit_y), span(q)].astype(F32) + t3[span(q)].astype(F32)
         wide = jnp.dot(unpack[...], total.astype(BF), preferred_element_type=F32)
         home[some(rows * per, q)] = wide.astype(BF)
-        loop(per * q, per * (q + 1), others(lambda c: deliver(c).start()))
+        deliver_all(q, lambda copy: copy.start())
 
     def step(q):
         finish(q)
@@ -365,8 +377,9 @@
     loop(1, CHUNKS, step)
     add_core(CHUNKS - 1)
     loop(0, CHUNKS, add_pair)
-    loop(0, CHUNKS, add_last)
-    last = pltpu.make_async_copy(home.at[some(rows, me)], spot(me), own_sem.at[1])
+    loop(1, CHUNKS, add_last)
+    add_last(0)
+    last = pltpu.make_async_copy(home.at[some(rows, mine)], spot(me), own_sem.at[1])
     last.start()
 
     def drain(q):
@@ -387,7 +400,7 @@
 
     loop(1, COLS, lambda k: put(k).wait_send())
     loop(0, CHUNKS, drain)
-    loop(0, COLS, others(lambda c: deliver(c).wait_send()))
+    loop(0, CHUNKS, lambda q: deliver_all(q, lambda copy: copy.wait_send()))
     loop(0, COLS, others(landed))
     last.wait()
 

time: 141 us -> 137 us (0.972)
  the two profiles are of different devices: /device:TPU:58 before, /device:TPU:2 now
where the time goes in v4:
time: 137 us
  Pallas kernels  126 us (92%)
  local copies, waits for them, and re-layouts  6.58 us (5%)
  matrix products  2.7 us (2%)
    pallas_call x1, Pallas kernels, body(): remote_call(layer_kernel, [VMEM_SPEC] + [pl.BlockSpec(memory_space=pl.ANY...  82.6 us
    pallas_call x1, Pallas kernels, body(): remote_call(gather_kernel, [VMEM_SPEC] * 2, (BLKS, 2, pairs, width), [dma...  25.5 us
    pallas_call x1, Pallas kernels, body(): remote_call(swap_kernel, [VMEM_SPEC], ((1, pairs, width), (1, pairs, widt...  18.2 us
    unnamed x12, local copies, waits for them, and re-layouts  3.28 us

profile of v4, /device:TPU:2, one launch (start us, length us, event | category | flops | bytes accessed | tf_op | source)
XLA Modules:
  0.0 136.9 jit_solution(17011350689750974752)
XLA Ops:
  0.6 0.0 copy-start.2
  0.6 0.0 copy-start.3
  0.7 0.0 copy-start
  0.7 0.6 copy-done.2
  1.3 0.0 copy-done.3
  1.3 0.1 fusion
  1.4 0.0 copy-done
  1.4 0.1 multiply_reduce_fusion
  1.5 0.1 gt.16
  1.6 0.2 copy.21
  1.9 0.1 copy.20
  1.9 0.1 copy.22
  2.0 0.2 and_select_fusion
  2.2 0.0 copy-start.4
  2.2 0.7 copy-done.4
  2.9 0.2 multiply_convert_fusion
  3.1 0.1 convert_element_type.32
  3.3 0.3 mul.82
  3.6 25.5 %shard_map.122 = bf16[16,2,2,4096]{3,2,1,0:T(2,128)(2,1)} custom-call(bf16[1,2,4096]{2,1,0:T(2,128)(2,1)} %x.1, bf16[1,2,4096]{2,1,0:T(2,128)(2,1)} %g.1), custom_call_target="tpu_custom_call" | custom-call | tf_op jit(solution)/shard_map/pallas_call | solution.py:458
  29.1 1.2 reshape.70
  30.3 1.1 convolution_convert_fusion.1.src
  31.4 82.6 %shard_map.123 = bf16[64,4096]{1,0:T(8,128)(2,1)} custom-call(bf16[64,4096]{1,0:T(8,128)(2,1)} %convolution_convert_fusion.1.src, bf16[1,128,4096]{2,1,0:T(8,128)(2,1)} %gate.1, bf16[1,128,4096]{2,1,0:T(8,128)(2,1)} %up.1, bf16[1,128,4096]{2,1,0:T(8,128)(2,1)} %down.1, bf16[2,96,64]{2,1,0:T(8,128)(2,1)} %constant.21.clone.pack, ...), custom_call_target="tpu_custom_call" | custom-call | tf_op jit(solution)/shard_map/pallas_call | solution.py:470
  114.0 1.6 %convolution_convert_fusion = bf16[64,4096]{1,0:T(8,128)(2,1)S(1)} fusion(f32[64,64]{0,1:T(8,128)S(1)} %mul.82, bf16[64,4096]{1,0:T(8,128)(2,1)} %shard_map.123), kind=kOutput, calls=%fused_computation | convolution fusion | flops 201588736 | bytes 1064960 | tf_op jit(solution)/shard_map/dot_general | solution.py:502
  115.6 1.1 reshape.71.src
  116.7 18.2 %shard_map.124 = (bf16[1,2,4096]{2,1,0:T(2,128)(2,1)}, bf16[1,2,4096]{2,1,0:T(2,128)(2,1)}) custom-call(bf16[16,2,2,4096]{3,2,1,0:T(2,128)(2,1)} %reshape.71.src), custom_call_target="tpu_custom_call" | custom-call | tf_op jit(solution)/shard_map/pallas_call | solution.py:506
  135.0 0.0 copy-start.1
  135.0 1.3 copy.25
  136.3 0.0 copy-done.1
  136.3 0.6 copy.26
  (3 shorter events, 0.0 us)
Async XLA Ops:
  0.6 0.7 copy-start.2
  0.6 0.7 copy-start.3
  0.7 0.8 copy-start
  2.2 0.7 copy-start.4
  135.0 1.4 copy-start.1

commit v5 on v4

--- a/solution.py
+++ b/solution.py
@@ -28,7 +28,7 @@
     lax.fori_loop(start, stop, run, 0)
 
 
-def greet(axis, me, n):
+def greet(axis, me, n, meanwhile):
     barrier = pltpu.get_barrier_semaphore()
     loop(
         1,
@@ -37,6 +37,7 @@
             barrier, inc=1, device_id={axis: lax.rem(me + k, n)}, device_id_type=MESH
         ),
     )
+    meanwhile()
     pl.semaphore_wait(barrier, n - 1)
 
 
@@ -146,13 +147,16 @@
 
 
 def layer_kernel(
-    src, gate, up, down, pack, unpack, out,
-    rows_ref, w, acc, og, t1, s1, t2, s2, t3, home,
+    both_ref, picks, gate, up, down, pack, unpack, out,
+    src, rows_ref, w, acc, acc_rest, og, t1, s1, t2, s2, t3, home,
     send_sem, recv_sem, own_sem, w_sem, hop_send, hop_recv,
     c_send, c_recv, y_send, y_recv, x_send, x_recv, h_send, h_recv,
 ):
     me = lax.axis_index("member")
-    width = src.shape[1] // SHARDS
+    width = both_ref.shape[1] // SHARDS
+    lane = width // 4
+    thin = width - lane
+    n = w.shape[0] // 3
     rows = 2 * PAD
     dense = 2 * CAP
     per = COLS // CHUNKS
@@ -163,24 +167,32 @@
     part_xy = flip(part_x, 4)
 
     loads = [
-        pltpu.make_async_copy(ref.at[0], w.at[i], w_sem.at[i])
+        pltpu.make_async_copy(ref.at[0], w.at[pl.ds(n * i, n)], w_sem.at[i])
         for i, ref in enumerate((gate, up, down))
     ]
     for load in loads:
         load.start()
-    greet("member", me, COLS)
-
     def some(size, at):
         return pl.ds(pl.multiple_of(size * at, size), size)
 
     def lanes(part):
         return some(width, part)
 
+    def pick(j):
+        sums = jnp.dot(picks[...], both_ref[:, lanes(j)], preferred_element_type=F32)
+        tall = src.shape[0]
+        for t in range(3):
+            tile = sums[:tall, lane * t : lane * (t + 1)]
+            tile = tile + sums[tall * (t + 1) : tall * (t + 2), thin:]
+            src[:, some(lane, 3 * j + t)] = tile.astype(BF)
+
+    greet("member", me, COLS, lambda: loop(0, SHARDS, pick))
+
     def piece(peer):
-        return src.at[some(rows, peer // SHARDS), lanes(lax.rem(peer, SHARDS))]
+        return src.at[some(rows, peer // SHARDS), some(thin, lax.rem(peer, SHARDS))]
 
     def place(col, part):
-        return rows_ref.at[some(rows, col), lanes(part)]
+        return rows_ref.at[some(rows, col), some(thin, part)]
 
     slot = me // SHARDS
 
@@ -215,7 +227,7 @@
         ).wait_recv()
 
     def hop(kind, q, origin, peer):
-        part = rows_ref.at[some(rows * per, chunk(q)), lanes(origin)]
+        part = rows_ref.at[some(rows * per, chunk(q)), some(thin, origin)]
         return send(part, part, hop_send.at[kind, q], hop_recv.at[kind, q], "member", peer)
 
     to_x = lambda q: hop(0, q, mine, across)
@@ -230,11 +242,17 @@
     core = lambda i, q: hop(3 + i, q, origins[i], other)
 
     def multiply(q, origin, fresh=False):
-        span, cols = some(rows * per, q), lanes(origin)
-        left = rows_ref[some(rows * per, chunk(q)), cols]
-        for i in range(3):
-            term = lax.dot_general(left, w[i, :, cols], NT, preferred_element_type=F32)
-            acc[i, span] = term if fresh else acc[i, span] + term
+        span = some(rows * per, q)
+        left = rows_ref[some(rows * per, chunk(q)), some(thin, origin)]
+        near = w[:, pl.ds(pl.multiple_of(width * origin, width), thin)]
+        rest = w[:, pl.ds(pl.multiple_of(width * origin + thin, lane), lane)]
+        term = lax.dot_general(left, near, NT, preferred_element_type=F32)
+        acc[span] = term if fresh else acc[span] + term
+        tiles = jnp.concatenate([left[:, lane * t : lane * (t + 1)] for t in range(3)], axis=0)
+        term = lax.dot_general(tiles, rest, NT, preferred_element_type=F32)
+        for t in range(3):
+            part = term[rows * per * t : rows * per * (t + 1)]
+            acc_rest[t, span] = part if fresh else acc_rest[t, span] + part
 
     own = pltpu.make_async_copy(piece(me), place(me, mine), own_sem.at[0])
     loop(1, COLS, lambda k: put(k).start())
@@ -277,11 +295,18 @@
         multiply(q, part_xy)
         core(3, q).wait_recv()
         multiply(q, flip(part_xy, 1))
-        n = w.shape[1]
-        split = [acc[i, some(rows * per, q)].reshape(per, 2, PAD, n) for i in range(3)]
-        pre_gate = split[0][:, 0].reshape(per * PAD, n)
-        pre_up = split[1][:, 0].reshape(per * PAD, n)
-        d_hidden = split[2][:, 1].reshape(per * PAD, n)
+        at = lax.broadcasted_iota(jnp.int32, (per, PAD, n), 1)
+
+        def whole(i, h):
+            cols = slice(n * i, n * (i + 1))
+            value = acc[some(rows * per, q), cols].reshape(per, 2, PAD, n)[:, h]
+            for t in range(3):
+                rest = acc_rest[t, some(rows * per, q), cols].reshape(per, 2, PAD, n)[:, h]
+                here = (at >= 2 * t) & (at < 2 * t + 2)
+                value = value + jnp.where(here, pltpu.roll(rest, 2 * t + 2, 1), 0.0)
+            return value.reshape(per * PAD, n)
+
+        pre_gate, pre_up, d_hidden = whole(0, 0), whole(1, 0), whole(2, 1)
         logistic = jax.nn.sigmoid(pre_gate)
         activated = pre_gate * logistic
         hidden = (activated * pre_up).astype(BF)
@@ -293,12 +318,11 @@
             jnp.dot(pack[h], v, preferred_element_type=F32).astype(BF)
             for h, v in ((1, grad_gate), (1, grad_up), (0, hidden))
         ]
+        left = jnp.concatenate(left, axis=1)
 
         def second(k):
             cols = lanes(k)
-            total = jnp.dot(left[0], w[0, :, cols], preferred_element_type=F32)
-            total += jnp.dot(left[1], w[1, :, cols], preferred_element_type=F32)
-            total += jnp.dot(left[2], w[2, :, cols], preferred_element_type=F32)
+            total = jnp.dot(left, w[:, cols], preferred_element_type=F32)
             og[some(dense * per, q), cols] = total.astype(BF)
 
         loop(0, SHARDS, second)
@@ -427,13 +451,19 @@
             for r in range(CAP):
                 pack[h, (c * 2 + h) * CAP + r, c * PAD + r] = 1
                 unpack[(c * 2 + h) * PAD + r, (c * 2 + h) * CAP + r] = 1
-    return jnp.asarray(pack, BF), jnp.asarray(unpack, BF)
+    spread = np.zeros((4, EXP_GRP * 2, PAD, EXP_GRP * 2, PAD), np.float32)
+    for e in range(EXP_GRP * 2):
+        for r in range(CAP):
+            spread[0, e, r, e, r] = 1
+            spread[1 + r // 2, e, CAP + r % 2, e, r] = 1
+    spread = spread.reshape(4 * EXP_GRP * 2 * PAD, EXP_GRP * 2 * PAD)
+    return jnp.asarray(pack, BF), jnp.asarray(unpack, BF), jnp.asarray(spread, BF)
 
 
 def body(tokens, cotangent, routes, gate_wts, w_gate, w_up, w_down):
     width = tokens.shape[2]
     dma = pltpu.SemaphoreType.DMA
-    pack, unpack = packing()
+    pack, unpack, spread = packing()
 
     experts = lax.axis_index("blk") * EXP_GRP + jnp.arange(EXP_GRP, dtype=jnp.int32)
     match = routes[0][None] == experts[:, None, None]
@@ -451,7 +481,7 @@
         grid = values.reshape(EXP_GRP, 1, PAD, BLKS, 1, COLS // BLKS) * both
         return grid.reshape(EXP_GRP * 2 * PAD, 2 * COLS)
 
-    picker = table(taken).astype(BF)
+    picks = jnp.dot(spread, table(taken).astype(BF), preferred_element_type=F32).astype(BF)
     combine = table(taken * weight[:, None, :]).T
 
     pairs = COLS // BLKS
@@ -462,19 +492,18 @@
         [dma((2, 8)), dma((2, 8)), dma((8,)), dma((8,))],
         0,
     )(tokens, cotangent)
-    picked = jnp.dot(
-        picker, column.reshape(2 * COLS, width), preferred_element_type=F32
-    ).astype(BF)
     dense, padded, piece = COLS * 2 * CAP, COLS * 2 * PAD, width // SHARDS
     hidden = w_gate.shape[1]
     sums = remote_call(
         layer_kernel,
-        [VMEM_SPEC] + [pl.BlockSpec(memory_space=pl.ANY)] * 3 + [VMEM_SPEC] * 2,
+        [VMEM_SPEC] * 2 + [pl.BlockSpec(memory_space=pl.ANY)] * 3 + [VMEM_SPEC] * 2,
         (EXP_GRP * 2 * PAD, width),
         [
-            pltpu.VMEM((padded, width), BF),
-            pltpu.VMEM((3, hidden, width), BF),
-            pltpu.VMEM((3, padded, hidden), F32),
+            pltpu.VMEM((EXP_GRP * 2 * PAD, width // 4 * 3), BF),
+            pltpu.VMEM((padded, width // 4 * 3), BF),
+            pltpu.VMEM((3 * hidden, width), BF),
+            pltpu.VMEM((padded, 3 * hidden), F32),
+            pltpu.VMEM((3, padded, 3 * hidden), F32),
             pltpu.VMEM((dense, width), BF),
             pltpu.VMEM((4, dense, piece), BF),
             pltpu.VMEM((4, dense, piece), BF),
@@ -498,7 +527,7 @@
             dma((COLS,)),
         ],
         1,
-    )(picked, w_gate, w_up, w_down, pack, unpack)
+    )(column.reshape(2 * COLS, width), picks, w_gate, w_up, w_down, pack, unpack)
     mixed = jnp.dot(
         combine, sums.astype(F32), precision=lax.Precision.HIGHEST, preferred_element_type=F32
     ).astype(BF)

time: 137 us -> 133 us (0.971)
  Pallas kernels: 126 us -> 121 us
  local copies, waits for them, and re-layouts: 6.58 us -> 8.81 us
    pallas_call x1, Pallas kernels: 82.6 us -> 77.2 us  [body(): remote_call(layer_kernel, [VMEM_SPEC] * 2 + [pl.BlockSpec(memory_space=pl...]
    unnamed x12 -> x14, local copies, waits for them, and re-layouts: 3.28 us -> 3.98 us
where the time goes in v5:
time: 133 us
  Pallas kernels  121 us (91%)
  local copies, waits for them, and re-layouts  8.81 us (7%)
  matrix products  1.73 us (1%)
    pallas_call x1, Pallas kernels, body(): remote_call(layer_kernel, [VMEM_SPEC] * 2 + [pl.BlockSpec(memory_space=pl...  77.2 us
    pallas_call x1, Pallas kernels, body(): remote_call(gather_kernel, [VMEM_SPEC] * 2, (BLKS, 2, pairs, width), [dma...  25.5 us
    pallas_call x1, Pallas kernels, body(): remote_call(swap_kernel, [VMEM_SPEC], ((1, pairs, width), (1, pairs, widt...  18.2 us
    unnamed x14, local copies, waits for them, and re-layouts  3.98 us

profile of v5, /device:TPU:2, one launch (start us, length us, event | category | flops | bytes accessed | tf_op | source)
XLA Modules:
  0.0 132.7 jit_solution(2939839042660714903)
XLA Ops:
  0.6 0.0 copy-start.3
  0.6 0.0 copy-start.4
  0.7 0.0 copy-start.1
  0.7 0.6 copy-done.3
  1.3 0.0 copy-done.4
  1.3 0.1 fusion
  1.4 0.0 copy-done.1
  1.4 0.1 multiply_reduce_fusion
  1.5 0.1 gt.16
  1.6 0.2 copy.26
  1.9 0.1 copy.25
  1.9 0.1 copy.27
  2.0 0.2 and_select_fusion
  2.2 0.0 copy-start.5
  2.2 0.7 copy-done.5
  2.9 0.2 multiply_convert_fusion
  3.1 0.0 copy-start
  3.1 0.1 convert_element_type.28
  3.3 0.7 copy-done
  4.0 0.1 convolution_convert_fusion.1
  4.1 0.8 copy.28
  4.9 0.3 mul.76
  5.2 25.5 %shard_map.131 = bf16[16,2,2,4096]{3,2,1,0:T(2,128)(2,1)} custom-call(bf16[1,2,4096]{2,1,0:T(2,128)(2,1)} %x.1, bf16[1,2,4096]{2,1,0:T(2,128)(2,1)} %g.1), custom_call_target="tpu_custom_call" | custom-call | tf_op jit(solution)/shard_map/pallas_call | solution.py:488
  30.7 2.0 %reshape.62.both_ref = bf16[64,4096]{1,0:T(8,128)(2,1)} reshape(bf16[16,2,2,4096]{3,2,1,0:T(2,128)(2,1)} %shard_map.131) | data formatting | bytes 1048576 | tf_op jit(solution)/shard_map/reshape | solution.py:530
  32.7 77.2 %shard_map.132 = bf16[64,4096]{1,0:T(8,128)(2,1)} custom-call(bf16[64,4096]{1,0:T(8,128)(2,1)} %reshape.62.both_ref, bf16[256,64]{1,0:T(8,128)(2,1)} %bitcast.13, bf16[1,128,4096]{2,1,0:T(8,128)(2,1)} %gate.1, bf16[1,128,4096]{2,1,0:T(8,128)(2,1)} %up.1, bf16[1,128,4096]{2,1,0:T(8,128)(2,1)} %down.1, bf16[2,96,64]{2,1,0:T(8,128)(2,1)} %constant.23.clone.pack, ...), custom_call_target="tpu_custom_call" | custom-call | tf_op jit(solution)/shard_map/pallas_call | solution.py:497
  109.8 1.6 %convolution_convert_fusion = bf16[64,4096]{1,0:T(8,128)(2,1)S(1)} fusion(f32[64,64]{0,1:T(8,128)S(1)} %mul.76, bf16[64,4096]{1,0:T(8,128)(2,1)} %shard_map.132), kind=kOutput, calls=%fused_computation | convolution fusion | flops 201588736 | bytes 1064960 | tf_op jit(solution)/shard_map/dot_general | solution.py:531
  111.4 1.1 reshape.63.src
  112.6 18.2 %shard_map.133 = (bf16[1,2,4096]{2,1,0:T(2,128)(2,1)}, bf16[1,2,4096]{2,1,0:T(2,128)(2,1)}) custom-call(bf16[16,2,2,4096]{3,2,1,0:T(2,128)(2,1)} %reshape.63.src), custom_call_target="tpu_custom_call" | custom-call | tf_op jit(solution)/shard_map/pallas_call | solution.py:535
  130.8 0.0 copy-start.2
  130.8 1.3 %copy.31 = bf16[1,2,4096]{2,1,0:T(2,128)(2,1)} copy(bf16[1,2,4096]{2,1,0:T(2,128)(2,1)} %get-tuple-element.10) | data formatting | bytes 32768
  132.1 0.0 copy-done.2
  132.1 0.6 copy.32
  (3 shorter events, 0.0 us)
Async XLA Ops:
  0.6 0.7 copy-start.3
  0.6 0.7 copy-start.4
  0.7 0.8 copy-start.1
  2.2 0.7 copy-start.5
  3.1 0.8 copy-start
  130.8 1.4 %copy-start.2 = (bf16[1,2,4096]{2,1,0:T(2,128)(2,1)S(1)}, bf16[1,2,4096]{2,1,0:T(2,128)(2,1)}, u32[]{:S(2)}) copy-start(bf16[1,2,4096]{2,1,0:T(2,128)(2,1)} %get-tuple-element.11) | copy-start | bytes 49156

commit v6 on v5

--- a/solution.py
+++ b/solution.py
@@ -52,14 +52,21 @@
     )
 
 
+def row_pairs():
+    pairs = COLS // BLKS
+    for i in range(2 * BLKS):
+        yield i // 2, i % 2, slice(pairs * i, pairs * (i + 1))
+
+
 def flip(m, w):
     return m + w - 2 * w * lax.rem(m // w, 2)
 
 
-def greet_few(axis, peers):
+def greet_few(axis, peers, meanwhile=lambda: None):
     barrier = pltpu.get_barrier_semaphore()
     for peer in peers:
         pl.semaphore_signal(barrier, inc=1, device_id={axis: peer}, device_id_type=MESH)
+    meanwhile()
     pl.semaphore_wait(barrier, len(peers))
 
 
@@ -107,11 +114,29 @@
         relay.wait()
 
 
-def swap_kernel(src, out_a, out_b, near, mid, far, send_sem, recv_sem, far_send, far_recv):
+def swap_kernel(
+    sums, combine, out_a, out_b, mixed, src, near, mid, far, send_sem, recv_sem, far_send, far_recv
+):
     me = lax.axis_index("blk")
     partner = flip(me, 1)
     ahead = {k: lax.rem(me + 2 * k, BLKS) for k in range(8)}
-    greet_few("blk", [ahead[k] for k in FAR_FIRST] + [partner])
+    width = sums.shape[1] // SHARDS
+
+    def mix(j):
+        cols = pl.ds(pl.multiple_of(width * j, width), width)
+        mixed[:, cols] = jnp.dot(
+            combine[...],
+            sums[:, cols].astype(F32),
+            precision=lax.Precision.HIGHEST,
+            preferred_element_type=F32,
+        )
+
+    def prepare():
+        loop(0, SHARDS, mix)
+        for p, h, at in row_pairs():
+            src[p, h] = mixed[at].astype(BF)
+
+    greet_few("blk", [ahead[k] for k in FAR_FIRST] + [partner], prepare)
 
     def pair(k):
         return send(
@@ -148,12 +173,12 @@
 
 def layer_kernel(
     both_ref, picks, gate, up, down, pack, unpack, out,
-    src, rows_ref, w, acc, acc_rest, og, t1, s1, t2, s2, t3, home,
+    flat, src, rows_ref, w, acc, acc_rest, og, t1, s1, t2, s2, t3, home,
     send_sem, recv_sem, own_sem, w_sem, hop_send, hop_recv,
     c_send, c_recv, y_send, y_recv, x_send, x_recv, h_send, h_recv,
 ):
     me = lax.axis_index("member")
-    width = both_ref.shape[1] // SHARDS
+    width = flat.shape[1] // SHARDS
     lane = width // 4
     thin = width - lane
     n = w.shape[0] // 3
@@ -179,14 +204,19 @@
         return some(width, part)
 
     def pick(j):
-        sums = jnp.dot(picks[...], both_ref[:, lanes(j)], preferred_element_type=F32)
+        sums = jnp.dot(picks[...], flat[:, lanes(j)].astype(BF), preferred_element_type=F32)
         tall = src.shape[0]
         for t in range(3):
             tile = sums[:tall, lane * t : lane * (t + 1)]
             tile = tile + sums[tall * (t + 1) : tall * (t + 2), thin:]
             src[:, some(lane, 3 * j + t)] = tile.astype(BF)
 
-    greet("member", me, COLS, lambda: loop(0, SHARDS, pick))
+    def regroup():
+        for p, h, at in row_pairs():
+            flat[at] = both_ref[p, h].astype(F32)
+        loop(0, SHARDS, pick)
+
+    greet("member", me, COLS, regroup)
 
     def piece(peer):
         return src.at[some(rows, peer // SHARDS), some(thin, lax.rem(peer, SHARDS))]
@@ -289,10 +319,12 @@
             other,
         )
 
-    def finish(q):
+    def near_done(q):
         relay(q).wait_recv()
         core(3, q).start()
         multiply(q, part_xy)
+
+    def finish(q):
         core(3, q).wait_recv()
         multiply(q, flip(part_xy, 1))
         at = lax.broadcasted_iota(jnp.int32, (per, PAD, n), 1)
@@ -335,6 +367,8 @@
     loop(0, CHUNKS, lambda q: multiply(q, mine, True))
     loop(0, CHUNKS, phase_near)
     loop(0, CHUNKS, phase_core)
+    near_done(0)
+    near_done(1)
     finish(0)
 
     def span(q):
@@ -395,10 +429,13 @@
         deliver_all(q, lambda copy: copy.start())
 
     def step(q):
-        finish(q)
-        add_core(q - 1)
-
-    loop(1, CHUNKS, step)
+        near_done(q)
+        finish(q - 1)
+        add_core(q - 2)
+
+    loop(2, CHUNKS, step)
+    finish(CHUNKS - 1)
+    add_core(CHUNKS - 2)
     add_core(CHUNKS - 1)
     loop(0, CHUNKS, add_pair)
     loop(1, CHUNKS, add_last)
@@ -499,6 +536,7 @@
         [VMEM_SPEC] * 2 + [pl.BlockSpec(memory_space=pl.ANY)] * 3 + [VMEM_SPEC] * 2,
         (EXP_GRP * 2 * PAD, width),
         [
+            pltpu.VMEM((2 * COLS, width), F32),
             pltpu.VMEM((EXP_GRP * 2 * PAD, width // 4 * 3), BF),
             pltpu.VMEM((padded, width // 4 * 3), BF),
             pltpu.VMEM((3 * hidden, width), BF),
@@ -527,18 +565,17 @@
             dma((COLS,)),
         ],
         1,
-    )(column.reshape(2 * COLS, width), picks, w_gate, w_up, w_down, pack, unpack)
-    mixed = jnp.dot(
-        combine, sums.astype(F32), precision=lax.Precision.HIGHEST, preferred_element_type=F32
-    ).astype(BF)
+    )(column, picks, w_gate, w_up, w_down, pack, unpack)
     half = (BLKS // 2, 2, pairs, width)
     return remote_call(
         swap_kernel,
-        [VMEM_SPEC],
+        [VMEM_SPEC] * 2,
         ((1, pairs, width), (1, pairs, width)),
-        [pltpu.VMEM(half, BF)] * 3 + [dma((8,))] * 4,
+        [pltpu.VMEM((2 * COLS, width), F32), pltpu.VMEM((BLKS, 2, pairs, width), BF)]
+        + [pltpu.VMEM(half, BF)] * 3
+        + [dma((8,))] * 4,
         2,
-    )(mixed.reshape(BLKS, 2, pairs, width))
+    )(sums, combine)
 
 
 def solution(mesh):

time: 133 us -> 127 us (0.955)
  local copies, waits for them, and re-layouts: 8.81 us -> 6.29 us
  Pallas kernels: 121 us -> 119 us
  matrix products: 1.73 us -> 0.13 us
    reshape x2 -> x0, local copies, waits for them, and re-layouts: 3.14 us -> none  [the longest x1 2.02 us: body(): column.reshape(2 * COLS, width)]
    pallas_call x1, Pallas kernels: 77.2 us -> 74.9 us  [body(): remote_call(layer_kernel, [VMEM_SPEC] * 2 + [pl.BlockSpec(memory_space=pl...]
    dot_general x1 -> x0, matrix products: 1.6 us -> none  [body(): jnp.dot(combine, sums.astype(F32), precision=lax.Precision.HIGHEST, prefe...]
where the time goes in v6:
time: 127 us; the launch traced here: 126 us
  Pallas kernels  119 us (94%)
  local copies, waits for them, and re-layouts  6.29 us (5%)
    pallas_call x1, Pallas kernels, body(): remote_call(layer_kernel, [VMEM_SPEC] * 2 + [pl.BlockSpec(memory_space=pl...  74.9 us
    pallas_call x1, Pallas kernels, body(): remote_call(gather_kernel, [VMEM_SPEC] * 2, (BLKS, 2, pairs, width), [dma...  25.5 us
    pallas_call x1, Pallas kernels, body(): remote_call(swap_kernel, [VMEM_SPEC] * 2, ((1, pairs, width), (1, pairs,...  18.3 us
    unnamed x14, local copies, waits for them, and re-layouts  3.99 us

profile of v6, /device:TPU:2, one launch (start us, length us, event | category | flops | bytes accessed | tf_op | source)
XLA Modules:
  0.0 126.5 jit_solution(15929984590574846354)
XLA Ops:
  0.6 0.0 copy-start.3
  0.6 0.0 copy-start.4
  0.7 0.0 copy-start.1
  0.7 0.6 copy-done.3
  1.3 0.0 copy-done.4
  1.3 0.1 fusion.1
  1.4 0.0 copy-done.1
  1.4 0.1 multiply_reduce_fusion
  1.5 0.1 gt.16
  1.6 0.2 copy.27
  1.9 0.1 copy.26
  1.9 0.1 copy.29
  2.0 0.2 broadcast_multiply_fusion.1
  2.2 0.0 copy-start.5
  2.2 0.7 copy-done.5
  2.9 0.2 broadcast_multiply_fusion
  3.1 0.9 mul.78
  4.0 0.0 copy-start
  4.0 0.1 convert_element_type.24
  4.2 0.7 copy-done
  4.9 0.1 convolution_convert_fusion
  5.0 0.8 copy.28
  5.8 25.5 %shard_map.131.both_ref = bf16[16,2,2,4096]{3,2,1,0:T(2,128)(2,1)} custom-call(bf16[1,2,4096]{2,1,0:T(2,128)(2,1)} %x.1, bf16[1,2,4096]{2,1,0:T(2,128)(2,1)} %g.1), custom_call_target="tpu_custom_call" | custom-call | tf_op jit(solution)/shard_map/pallas_call | solution.py:525
  31.3 74.9 %shard_map.132.sums = bf16[64,4096]{1,0:T(8,128)(2,1)} custom-call(bf16[16,2,2,4096]{3,2,1,0:T(2,128)(2,1)} %shard_map.131.both_ref, bf16[256,64]{1,0:T(8,128)(2,1)} %bitcast.12, bf16[1,128,4096]{2,1,0:T(8,128)(2,1)} %gate.1, bf16[1,128,4096]{2,1,0:T(8,128)(2,1)} %up.1, bf16[1,128,4096]{2,1,0:T(8,128)(2,1)} %down.1, bf16[2,96,64]{2,1,0:T(8,128)(2,1)} %constant.23.clone.pack, ...), custom_call_target="tpu_custom_call" | custom-call | tf_op jit(solution)/shard_map/pallas_call | solution.py:534
  106.2 18.3 %shard_map.133 = (bf16[1,2,4096]{2,1,0:T(2,128)(2,1)}, bf16[1,2,4096]{2,1,0:T(2,128)(2,1)}) custom-call(bf16[64,4096]{1,0:T(8,128)(2,1)} %shard_map.132.sums, f32[64,64]{1,0:T(8,128)} %bitcast.13), custom_call_target="tpu_custom_call" | custom-call | tf_op jit(solution)/shard_map/pallas_call | solution.py:570
  124.5 0.0 copy-start.2
  124.5 1.3 %copy.32 = bf16[1,2,4096]{2,1,0:T(2,128)(2,1)} copy(bf16[1,2,4096]{2,1,0:T(2,128)(2,1)} %get-tuple-element.10) | data formatting | bytes 32768
  125.9 0.0 copy-done.2
  125.9 0.6 copy.33
  (3 shorter events, 0.0 us)
Async XLA Ops:
  0.6 0.7 copy-start.3
  0.6 0.7 copy-start.4
  0.7 0.8 copy-start.1
  2.2 0.7 copy-start.5
  4.0 0.8 copy-start
  124.5 1.4 %copy-start.2 = (bf16[1,2,4096]{2,1,0:T(2,128)(2,1)S(1)}, bf16[1,2,4096]{2,1,0:T(2,128)(2,1)}, u32[]{:S(2)}) copy-start(bf16[1,2,4096]{2,1,0:T(2,128)(2,1)} %get-tuple-element.11) | copy-start | bytes 49156

commit v7 on v6

--- a/solution.py
+++ b/solution.py
@@ -172,8 +172,8 @@
 
 
 def layer_kernel(
-    both_ref, picks, gate, up, down, pack, unpack, out,
-    flat, src, rows_ref, w, acc, acc_rest, og, t1, s1, t2, s2, t3, home,
+    both_ref, picker, gate, up, down, pack, unpack, spread, out,
+    picks, flat, src, rows_ref, w, acc, acc_rest, og, t1, s1, t2, s2, t3, home,
     send_sem, recv_sem, own_sem, w_sem, hop_send, hop_recv,
     c_send, c_recv, y_send, y_recv, x_send, x_recv, h_send, h_recv,
 ):
@@ -214,6 +214,7 @@
     def regroup():
         for p, h, at in row_pairs():
             flat[at] = both_ref[p, h].astype(F32)
+        picks[...] = jnp.dot(spread[...], picker[...], preferred_element_type=F32).astype(BF)
         loop(0, SHARDS, pick)
 
     greet("member", me, COLS, regroup)
@@ -301,6 +302,9 @@
         to_y(q).wait_recv()
         relay(q).start()
         core(2, q).start()
+
+    def first_blocks(q):
+        multiply(q, mine, True)
         multiply(q, part_x)
         multiply(q, part_y)
 
@@ -362,10 +366,10 @@
             swap_core(q, h).start()
 
     loop(0, CHUNKS, phase_own)
+    loop(0, CHUNKS, phase_near)
     for load in loads:
         load.wait()
-    loop(0, CHUNKS, lambda q: multiply(q, mine, True))
-    loop(0, CHUNKS, phase_near)
+    loop(0, CHUNKS, first_blocks)
     loop(0, CHUNKS, phase_core)
     near_done(0)
     near_done(1)
@@ -506,8 +510,9 @@
     match = routes[0][None] == experts[:, None, None]
     named = jnp.sum(match.astype(F32), axis=2)
     weight = jnp.sum(jnp.where(match, gate_wts[0][None], 0.0), axis=2)
-    earlier = np.tril(np.ones((COLS, COLS), np.float32), -1)
-    rank = jnp.sum(named[:, None, :] * earlier[None], axis=2)
+    square = (EXP_GRP, COLS, COLS)
+    earlier = lax.broadcasted_iota(jnp.int32, square, 2) < lax.broadcasted_iota(jnp.int32, square, 1)
+    rank = jnp.sum(jnp.where(earlier, named[:, None, :], 0.0), axis=2)
     places = jnp.arange(PAD, dtype=jnp.int32).astype(F32)
     taken = jnp.where(
         (rank[:, None, :] == places[None, :, None]) & (named[:, None, :] > 0), 1.0, 0.0
@@ -518,7 +523,7 @@
         grid = values.reshape(EXP_GRP, 1, PAD, BLKS, 1, COLS // BLKS) * both
         return grid.reshape(EXP_GRP * 2 * PAD, 2 * COLS)
 
-    picks = jnp.dot(spread, table(taken).astype(BF), preferred_element_type=F32).astype(BF)
+    picker = table(taken).astype(BF)
     combine = table(taken * weight[:, None, :]).T
 
     pairs = COLS // BLKS
@@ -533,9 +538,10 @@
     hidden = w_gate.shape[1]
     sums = remote_call(
         layer_kernel,
-        [VMEM_SPEC] * 2 + [pl.BlockSpec(memory_space=pl.ANY)] * 3 + [VMEM_SPEC] * 2,
+        [VMEM_SPEC] * 2 + [pl.BlockSpec(memory_space=pl.ANY)] * 3 + [VMEM_SPEC] * 3,
         (EXP_GRP * 2 * PAD, width),
         [
+            pltpu.VMEM((8 * EXP_GRP * PAD, 2 * COLS), BF),
             pltpu.VMEM((2 * COLS, width), F32),
             pltpu.VMEM((EXP_GRP * 2 * PAD, width // 4 * 3), BF),
             pltpu.VMEM((padded, width // 4 * 3), BF),
@@ -565,7 +571,7 @@
             dma((COLS,)),
         ],
         1,
-    )(column, picks, w_gate, w_up, w_down, pack, unpack)
+    )(column, picker, w_gate, w_up, w_down, pack, unpack, spread)
     half = (BLKS // 2, 2, pairs, width)
     return remote_call(
         swap_kernel,

time: 127 us -> 129 us (1.016)
  the two profiles are of different devices: /device:TPU:2 before, /device:TPU:18 now
where the time goes in v7:
time: 129 us; the launch traced here: 128 us
  Pallas kernels  121 us (94%)
  local copies, waits for them, and re-layouts  5.52 us (4%)
    pallas_call x1, Pallas kernels, body(): remote_call(layer_kernel, [VMEM_SPEC] * 2 + [pl.BlockSpec(memory_space=pl...  77 us
    pallas_call x1, Pallas kernels, body(): remote_call(gather_kernel, [VMEM_SPEC] * 2, (BLKS, 2, pairs, width), [dma...  25.5 us
    pallas_call x1, Pallas kernels, body(): remote_call(swap_kernel, [VMEM_SPEC] * 2, ((1, pairs, width), (1, pairs,...  18.9 us
    unnamed x10, local copies, waits for them, and re-layouts  3.29 us

profile of v7, /device:TPU:18, one launch (start us, length us, event | category | flops | bytes accessed | tf_op | source)
XLA Modules:
  0.0 128.3 jit_solution(1138721986943504485)
XLA Ops:
  0.6 0.0 copy-start.2
  0.6 0.0 copy-start.1
  0.7 0.6 copy-done.2
  1.3 0.0 copy-done.1
  1.3 0.1 fusion.1
  1.4 0.1 select_reduce_fusion
  1.5 0.1 gt.16
  1.6 0.2 copy.22
  1.9 0.1 copy.21
  1.9 0.1 copy.24
  2.0 0.2 broadcast_multiply_fusion.1
  2.2 0.0 copy-start.3
  2.2 0.7 copy-done.3
  2.9 0.2 broadcast_multiply_fusion
  3.1 0.9 mul.59
  4.0 0.1 convert_element_type.18
  4.2 0.7 copy.23.picker
  4.9 25.5 %shard_map.122.both_ref = bf16[16,2,2,4096]{3,2,1,0:T(2,128)(2,1)} custom-call(bf16[1,2,4096]{2,1,0:T(2,128)(2,1)} %x.1, bf16[1,2,4096]{2,1,0:T(2,128)(2,1)} %g.1), custom_call_target="tpu_custom_call" | custom-call | tf_op jit(solution)/shard_map/pallas_call | solution.py:530
  30.4 77.0 %shard_map.123.sums = bf16[64,4096]{1,0:T(8,128)(2,1)} custom-call(bf16[16,2,2,4096]{3,2,1,0:T(2,128)(2,1)} %shard_map.122.both_ref, bf16[64,64]{1,0:T(8,128)(2,1)} %copy.23.picker, bf16[1,128,4096]{2,1,0:T(8,128)(2,1)} %gate.1, bf16[1,128,4096]{2,1,0:T(8,128)(2,1)} %up.1, bf16[1,128,4096]{2,1,0:T(8,128)(2,1)} %down.1, ...), custom_call_target="tpu_custom_call" | custom-call | tf_op jit(solution)/shard_map/pallas_call | solution.py:539
  107.4 18.9 %shard_map.124 = (bf16[1,2,4096]{2,1,0:T(2,128)(2,1)}, bf16[1,2,4096]{2,1,0:T(2,128)(2,1)}) custom-call(bf16[64,4096]{1,0:T(8,128)(2,1)} %shard_map.123.sums, f32[64,64]{1,0:T(8,128)} %bitcast.9), custom_call_target="tpu_custom_call" | custom-call | tf_op jit(solution)/shard_map/pallas_call | solution.py:576
  126.3 0.0 copy-start
  126.3 1.3 %copy.27 = bf16[1,2,4096]{2,1,0:T(2,128)(2,1)} copy(bf16[1,2,4096]{2,1,0:T(2,128)(2,1)} %get-tuple-element.10) | data formatting | bytes 32768
  127.7 0.0 copy-done
  127.7 0.6 copy.28
  (3 shorter events, 0.0 us)
Async XLA Ops:
  0.6 0.7 copy-start.2
  0.6 0.7 copy-start.1
  2.2 0.7 copy-start.3
  126.3 1.4 %copy-start = (bf16[1,2,4096]{2,1,0:T(2,128)(2,1)S(1)}, bf16[1,2,4096]{2,1,0:T(2,128)(2,1)}, u32[]{:S(2)}) copy-start(bf16[1,2,4096]{2,1,0:T(2,128)(2,1)} %get-tuple-element.11) | copy-start | bytes 49156

commit v8 on v7

--- a/solution.py
+++ b/solution.py
@@ -295,6 +295,7 @@
         to_x(q).start()
         to_y(q).start()
         core(0, q).start()
+        multiply(q, mine, True)
 
     def phase_near(q):
         to_x(q).wait_recv()
@@ -302,9 +303,6 @@
         to_y(q).wait_recv()
         relay(q).start()
         core(2, q).start()
-
-    def first_blocks(q):
-        multiply(q, mine, True)
         multiply(q, part_x)
         multiply(q, part_y)
 
@@ -365,11 +363,10 @@
         for h in range(4):
             swap_core(q, h).start()
 
+    for load in loads:
+        load.wait()
     loop(0, CHUNKS, phase_own)
     loop(0, CHUNKS, phase_near)
-    for load in loads:
-        load.wait()
-    loop(0, CHUNKS, first_blocks)
     loop(0, CHUNKS, phase_core)
     near_done(0)
     near_done(1)

time: 129 us -> 127 us (0.984)
  Pallas kernels: 121 us -> 119 us
    pallas_call x1, Pallas kernels: 77 us -> 75 us  [body(): remote_call(layer_kernel, [VMEM_SPEC] * 2 + [pl.BlockSpec(memory_space=pl...]
where the time goes in v8:
time: 127 us; the launch traced here: 126 us
  Pallas kernels  119 us (94%)
  local copies, waits for them, and re-layouts  5.52 us (4%)
    pallas_call x1, Pallas kernels, body(): remote_call(layer_kernel, [VMEM_SPEC] * 2 + [pl.BlockSpec(memory_space=pl...  75 us
    pallas_call x1, Pallas kernels, body(): remote_call(gather_kernel, [VMEM_SPEC] * 2, (BLKS, 2, pairs, width), [dma...  25.5 us
    pallas_call x1, Pallas kernels, body(): remote_call(swap_kernel, [VMEM_SPEC] * 2, ((1, pairs, width), (1, pairs,...  18.9 us
    unnamed x10, local copies, waits for them, and re-layouts  3.29 us

profile of v8, /device:TPU:18, one launch (start us, length us, event | category | flops | bytes accessed | tf_op | source)
XLA Modules:
  0.0 126.2 jit_solution(15722831982660129630)
XLA Ops:
  0.6 0.0 copy-start.2
  0.6 0.0 copy-start.1
  0.7 0.6 copy-done.2
  1.3 0.0 copy-done.1
  1.3 0.1 fusion.1
  1.4 0.1 select_reduce_fusion
  1.5 0.1 gt.16
  1.6 0.2 copy.22
  1.9 0.1 copy.21
  1.9 0.1 copy.24
  2.0 0.2 broadcast_multiply_fusion.1
  2.2 0.0 copy-start.3
  2.2 0.7 copy-done.3
  2.9 0.2 broadcast_multiply_fusion
  3.1 0.9 mul.59
  4.0 0.1 convert_element_type.18
  4.2 0.7 copy.23.picker
  4.9 25.5 %shard_map.122.both_ref = bf16[16,2,2,4096]{3,2,1,0:T(2,128)(2,1)} custom-call(bf16[1,2,4096]{2,1,0:T(2,128)(2,1)} %x.1, bf16[1,2,4096]{2,1,0:T(2,128)(2,1)} %g.1), custom_call_target="tpu_custom_call" | custom-call | tf_op jit(solution)/shard_map/pallas_call | solution.py:527
  30.4 75.0 %shard_map.123.sums = bf16[64,4096]{1,0:T(8,128)(2,1)} custom-call(bf16[16,2,2,4096]{3,2,1,0:T(2,128)(2,1)} %shard_map.122.both_ref, bf16[64,64]{1,0:T(8,128)(2,1)} %copy.23.picker, bf16[1,128,4096]{2,1,0:T(8,128)(2,1)} %gate.1, bf16[1,128,4096]{2,1,0:T(8,128)(2,1)} %up.1, bf16[1,128,4096]{2,1,0:T(8,128)(2,1)} %down.1, ...), custom_call_target="tpu_custom_call" | custom-call | tf_op jit(solution)/shard_map/pallas_call | solution.py:536
  105.3 18.9 %shard_map.124 = (bf16[1,2,4096]{2,1,0:T(2,128)(2,1)}, bf16[1,2,4096]{2,1,0:T(2,128)(2,1)}) custom-call(bf16[64,4096]{1,0:T(8,128)(2,1)} %shard_map.123.sums, f32[64,64]{1,0:T(8,128)} %bitcast.9), custom_call_target="tpu_custom_call" | custom-call | tf_op jit(solution)/shard_map/pallas_call | solution.py:573
  124.3 0.0 copy-start
  124.3 1.3 %copy.27 = bf16[1,2,4096]{2,1,0:T(2,128)(2,1)} copy(bf16[1,2,4096]{2,1,0:T(2,128)(2,1)} %get-tuple-element.10) | data formatting | bytes 32768
  125.6 0.0 copy-done
  125.6 0.6 copy.28
  (3 shorter events, 0.0 us)
Async XLA Ops:
  0.6 0.7 copy-start.2
  0.6 0.7 copy-start.1
  2.2 0.7 copy-start.3
  124.3 1.4 %copy-start = (bf16[1,2,4096]{2,1,0:T(2,128)(2,1)S(1)}, bf16[1,2,4096]{2,1,0:T(2,128)(2,1)}, u32[]{:S(2)}) copy-start(bf16[1,2,4096]{2,1,0:T(2,128)(2,1)} %get-tuple-element.11) | copy-start | bytes 49156
